TPU v7x, 256 devices: a whole 4x4x8 slice. The times are simulated.
256 devices in a mesh: hx: 32 (over x, y, core), nb: 8 (over z).
Axes of the slice: x: 4, y: 4, z: 8, core: 2. Of those that a mesh axis runs over, the one named last changes fastest.
Arguments:
- partial_multipoles: bfloat16 [8, 16384, 1464], P('nb', 'hx'), may hold values from -6 to 6
- shared_slots: int32 [8, 16384], P('nb', 'hx'), may hold values from -1 to 1023, as said below
- m2l_sources: int32 [8, 2, 32768], P('nb', None, 'hx'), may hold values from 0 to 1023
- m2l_ops: bfloat16 [2, 1464, 1464], replicated, may hold values from -0.15625 to 0.15625
- positions: float32 [8, 3, 65536], P('nb', None, 'hx'), may hold values from -1 to 1
- forces: float32 [8, 3, 65536], P('nb', None, 'hx'), may hold values from -6 to 6
- leaf_counts: int32 [8, 512], P('nb', 'hx'), may hold values from 32 to 128
- neighbours: int32 [8, 8, 512], P('nb', None, 'hx'), may hold values from 0 to 47
Outputs:
- local_expansion: bfloat16 [8, 32768, 1464], P('nb', 'hx')
- velocity: float32 [8, 3, 65536], P('nb', None, 'hx')
Inputs may be any that keep to these rules, and one draw needn't show every extreme that they name: `shared_slots`: rows j * 16 to (j + 1) * 16 - 1 of each device's 512 rows belong to owner j along hx. Each such block names exactly 4 distinct octants, each at least once; its other rows name one of these or are -1.
All inputs are finite; a program needn't handle non-finite values.
Results may differ from a plain program's by a relative error of at most 0.0048.
Values may be sent and summed in bfloat16 or wider, within the bound.
A program may use at most 64 MiB of HBM per device.

v0:
```python
import math

import jax
import jax.numpy as jnp
from jax import lax
from jax.sharding import PartitionSpec as P

reg_eps2 = 0.01
inv_eight_pi = 1.0 / (8.0 * math.pi)


def padded(x, sides, width):
    for axis, dim in sides:
        devices, length = (lax.axis_size(axis), x.shape[dim])
        up = [(i, (i + 1) % devices) for i in range(devices - 1)]
        down = [(j, i) for i, j in up]
        last = lax.slice_in_dim(x, length - width, length, axis=dim)
        leading = lax.slice_in_dim(x, 0, width, axis=dim)
        before = lax.ppermute(last, axis, up)
        after = lax.ppermute(leading, axis, down)
        x = jnp.concatenate([before, x, after], axis=dim)
    return x


def leaf_velocity(target_pos, target_live, source_pos, source_frc):
    offset = target_pos[:, None, :] - source_pos[:, :, None]
    dist_sq = jnp.sum(offset * offset, axis=0) + reg_eps2
    inverse_cube = 1.0 / (dist_sq * jnp.sqrt(dist_sq))
    projected = jnp.sum(source_frc[:, :, None] * offset, axis=0)
    summand = (
        source_frc[:, :, None] * (dist_sq + reg_eps2)[None] + projected[None] * offset
    ) * inverse_cube[None]
    return jnp.sum(summand, axis=1) * inv_eight_pi * target_live[None, :]


def leaves_block(own_pos, own_live, leaf_lists, source_table):

    def one_leaf(item):
        leaf_pos, leaf_live, leaf_list = item
        chosen = source_table[:, leaf_list, :].reshape(6, -1)
        return leaf_velocity(leaf_pos, leaf_live, chosen[:3], chosen[3:])

    result = lax.map(one_leaf, (own_pos.transpose(1, 0, 2), own_live, leaf_lists.T))
    return result.transpose(1, 0, 2)


def on_device(
    partial_multipoles,
    shared_slots,
    m2l_sources,
    m2l_ops,
    positions,
    forces,
    leaf_counts,
    neighbours,
):
    hx_count = lax.axis_size("hx")
    shard_rows = partial_multipoles[0]
    coeff_width = shard_rows.shape[1]
    slot_cap = shard_rows.shape[0] // hx_count
    owned = m2l_sources.shape[2]
    slot_rows = shard_rows.reshape(hx_count, slot_cap, coeff_width)
    slot_ids = shared_slots[0].reshape(hx_count, slot_cap)
    octant_range = jnp.arange(owned, dtype=jnp.int32)
    arrived = lax.all_to_all(slot_rows, "hx", split_axis=0, concat_axis=0, tiled=True)
    arrived_ids = lax.all_to_all(slot_ids, "hx", split_axis=0, concat_axis=0, tiled=True)
    one_hot = (arrived_ids.reshape(-1)[None, :] == octant_range[:, None]).astype(jnp.bfloat16)
    summed = jnp.dot(one_hot, arrived.reshape(-1, coeff_width), preferred_element_type=jnp.float32)
    multipoles = summed.astype(jnp.bfloat16)
    total = jnp.zeros((owned, coeff_width), jnp.float32)
    for direction in range(m2l_ops.shape[0]):
        picked = multipoles[m2l_sources[0, direction]]
        total = total + jnp.dot(picked, m2l_ops[direction], preferred_element_type=jnp.float32)
    local_expansion = total.astype(jnp.bfloat16)[None]
    leaf_total = leaf_counts.shape[1]
    per_leaf = positions.shape[2] // leaf_total
    live_mask = (jnp.arange(per_leaf, dtype=jnp.int32)[None, :] < leaf_counts[0][:, None]).astype(
        jnp.float32
    )
    own_pos = positions[0].reshape(3, leaf_total, per_leaf)
    own_frc = forces[0].reshape(3, leaf_total, per_leaf) * live_mask[None]
    packed = jnp.concatenate([own_pos, own_frc], axis=0)[None]
    extended = padded(packed, (("nb", 0),), 1)
    source_table = extended.transpose(1, 0, 2, 3).reshape(6, 3 * leaf_total, per_leaf)
    result = leaves_block(own_pos, live_mask, neighbours[0], source_table)
    velocity = result.reshape(3, leaf_total * per_leaf)[None]
    return (local_expansion, velocity)


def solution(mesh):
    placed = (
        P("nb", "hx", None),
        P("nb", "hx"),
        P("nb", None, "hx"),
        P(),
        P("nb", None, "hx"),
        P("nb", None, "hx"),
        P("nb", "hx"),
        P("nb", None, "hx"),
    )
    return jax.shard_map(
        on_device,
        mesh=mesh,
        in_specs=placed,
        out_specs=(P("nb", "hx", None), P("nb", None, "hx")),
        check_vma=False,
    )
```

profile of v0, /device:TPU:1, one launch (start us, length us, event | category | flops | bytes accessed | tf_op | source)
XLA Modules:
  0.0 124.7 jit_solution(17211743345535751409)
XLA Ops:
  2.9 1.3 %collective-permute-start.1 = (f32[1,6,16,128]{3,2,1,0:T(8,128)S(1)}, f32[1,6,16,128]{3,2,1,0:T(8,128)S(1)}, u32[]{:S(2)}, u32[]{:S(2)}) collective-permute-start(f32[1,6,16,128]{3,2,1,0:T(8,128)S(1)} %maximum_bitcast_fusion.1), channel_id=1, source_target_pairs={{1,0},{2,1},{3,2},{4,3},{5,4},{6,5},{7,6},{9,8},{10,9},{11,10},{12... | collective-permute-start | bytes 147464 | tf_op jit(solution)/shard_map/ppermute | solution.py:20
  4.1 5.0 %collective-permute-start = (f32[1,6,16,128]{3,2,1,0:T(8,128)S(1)}, f32[1,6,16,128]{3,2,1,0:T(8,128)S(1)}, u32[]{:S(2)}, u32[]{:S(2)}) collective-permute-start(f32[1,6,16,128]{3,2,1,0:T(8,128)S(1)} %maximum_bitcast_fusion.1), channel_id=1, source_target_pairs={{0,1},{1,2},{2,3},{3,4},{4,5},{5,6},{6,7},{8,9},{9,10},{10,11},{11... | collective-permute-start | bytes 147464 | tf_op jit(solution)/shard_map/ppermute | solution.py:19
  9.6 1.3 %reduce.6 = s32[512]{0:T(512)S(1)} reduce(s32[1,512]{1,0:T(1,128)} %param.11, s32[]{:T(128)} %broadcast.161), dimensions={0}, to_apply=%param.11.reduce_sub_computation.3 | reduce | bytes 4100 | tf_op args[1]
  11.6 8.1 %all-to-all-start = ((s32[32,1,16]{2,1,0:T(1,128)}), s32[32,1,16]{2,1,0:T(1,128)S(1)}, u32[]{:S(2)}, u32[]{:S(2)}) async-start(s32[32,1,16]{2,1,0:T(1,128)} %bitcast.8), calls=%async_computation | async-start | bytes 32768 | tf_op jit(solution)/shard_map/all_to_all | solution.py:66
  20.6 2.6 %copy.32 = bf16[1,512,1464]{2,1,0:T(8,128)(2,1)} copy(bf16[1,512,1464]{1,2,0:T(8,128)(2,1)} %param.10) | data formatting | bytes 2998272 | tf_op args[0]
  23.2 3.4 %all-to-all-done = s32[32,1,16]{2,1,0:T(1,128)S(1)} async-done(((s32[32,1,16]{2,1,0:T(1,128)}), s32[32,1,16]{2,1,0:T(1,128)S(1)}, u32[]{:S(2)}, u32[]{:S(2)}) %all-to-all-start) | async-done | bytes 2080 | tf_op jit(solution)/shard_map/all_to_all | solution.py:66
  26.6 4.3 %all-to-all-start.1 = ((bf16[32,16,1464]{2,1,0:T(8,128)(2,1)}), bf16[32,16,1464]{2,1,0:T(8,128)(2,1)S(1)}, u32[]{:S(2)}, u32[]{:S(2)}) async-start(bf16[32,16,1464]{2,1,0:T(8,128)(2,1)} %bitcast.9), calls=%async_computation.1 | async-start | bytes 3145728 | tf_op jit(solution)/shard_map/all_to_all | solution.py:65
  31.7 57.8 %while.12 = (s32[]{:T(128)}, f32[16,3,128]{2,1,0:T(4,128)S(1)}, s32[16,8]{1,0:T(8,128)S(1)}, f32[6,48,128]{2,0,1:T(8,128)S(1)}, f32[16,3,128]{2,0,1:T(8,128)}, /*index=5*/f32[16,128]{1,0:T(8,128)S(1)}, s32[]{:T(128)}) while((s32[]{:T(128)}, f32[16,3,128]{2,1,0:T(4,128)S(1)}, s32[16,8]{1,0:T(8,128)S(1)}, f32[6,48,128]{2,0,1:T(8,128)S(1)}, ...), condition=%wide.region_4.5_spmd, body=%wide.region_0.4_spmd.sunk | while | flops 4588698 | bytes 4362469 | solution.py:43
  33.1 1.0 fusion.33
  36.7 1.0 fusion.33
  40.3 1.0 fusion.33
  43.9 1.0 fusion.33
  45.1 1.0 fusion.34
  47.5 1.0 fusion.33
  48.8 1.0 fusion.34
  51.1 1.0 fusion.33
  54.8 1.0 fusion.33
  58.4 1.0 fusion.33
  62.0 1.0 fusion.33
  65.6 1.0 fusion.33
  69.2 1.0 fusion.33
  72.8 1.0 fusion.33
  76.4 1.0 fusion.33
  80.0 1.0 fusion.33
  83.7 1.0 fusion.33
  87.3 1.0 fusion.33
  90.2 3.4 %convolution_convert_fusion = bf16[1024,1464]{0,1:T(8,128)(2,1)} fusion(bf16[512,1464]{1,0:T(8,128)(2,1)S(1)} %bitcast.76, s32[512]{0:T(512)S(1)} %eq.15), kind=kOutput, calls=%fused_computation.35 | convolution fusion | flops 1537138688 | bytes 4499456 | tf_op jit(solution)/shard_map/dot_general | solution.py:68
  93.6 3.1 %copy.33 = bf16[1024,1464]{1,0:T(8,128)(2,1)S(1)} copy(bf16[1024,1464]{0,1:T(8,128)(2,1)} %convolution_convert_fusion) | data formatting | bytes 5996544 | tf_op jit(solution)/shard_map/convert_element_type | solution.py:69
  96.7 5.6 %gather_fusion.2 = bf16[1024,1464]{1,0:T(8,128)(2,1)} fusion(bf16[1024,1464]{1,0:T(8,128)(2,1)S(1)} %copy.33, s32[1024]{0:T(1024)S(1)} %broadcast_clamp_fusion), kind=kCustom, calls=%fused_computation.2 | custom fusion | bytes 6000640 | tf_op jit(solution)/shard_map/gather | solution.py:72
  102.3 5.6 %gather_fusion.1 = bf16[1024,1464]{1,0:T(8,128)(2,1)} fusion(bf16[1024,1464]{1,0:T(8,128)(2,1)S(1)} %copy.33, s32[1024]{0:T(1024)S(1)} %broadcast_clamp_fusion.1), kind=kCustom, calls=%fused_computation.1 | custom fusion | bytes 6000640 | tf_op jit(solution)/shard_map/gather | solution.py:72
  107.9 8.2 %fusion.11 = f32[1024,1464]{0,1:T(8,128)S(1)} fusion(bf16[1024,1464]{1,0:T(8,128)(2,1)} %gather_fusion.2, bf16[2,1464,1464]{2,1,0:T(8,128)(2,1)} %param.13), kind=kOutput, calls=%fused_computation.29 | convolution fusion | flops 4389470208 | bytes 13639680 | tf_op jit(solution)/shard_map/dot_general | solution.py:73
  116.2 8.5 %fusion.19 = bf16[1,1024,1464]{1,2,0:T(8,128)(2,1)} fusion(f32[1024,1464]{0,1:T(8,128)S(1)} %fusion.11, bf16[1024,1464]{1,0:T(8,128)(2,1)S(1)} %copy-done, bf16[2,1464,1464]{2,1,0:T(8,128)(2,1)} %param.13), kind=kOutput, calls=%fused_computation.36 | convolution fusion | flops 4392468480 | bytes 16490496 | tf_op jit(solution)/shard_map/dot_general | solution.py:73
  (181 shorter events, 44.0 us)
Async XLA Ops:
  0.6 22.5 %copy-start.1 = (s32[1,8,16]{2,1,0:T(8,128)S(1)}, s32[1,8,16]{2,1,0:T(8,128)}, u32[]{:S(2)}) copy-start(s32[1,8,16]{2,1,0:T(8,128)} %param.17) | copy-start | bytes 1540
  2.9 28.8 %collective-permute-start.1 = (f32[1,6,16,128]{3,2,1,0:T(8,128)S(1)}, f32[1,6,16,128]{3,2,1,0:T(8,128)S(1)}, u32[]{:S(2)}, u32[]{:S(2)}) collective-permute-start(f32[1,6,16,128]{3,2,1,0:T(8,128)S(1)} %maximum_bitcast_fusion.1), channel_id=1, source_target_pairs={{1,0},{2,1},{3,2},{4,3},{5,4},{6,5},{7,6},{9,8},{10,9},{11,10},{12... | collective-permute-start | bytes 147464 | tf_op jit(solution)/shard_map/ppermute | solution.py:20
  4.1 27.5 %collective-permute-start = (f32[1,6,16,128]{3,2,1,0:T(8,128)S(1)}, f32[1,6,16,128]{3,2,1,0:T(8,128)S(1)}, u32[]{:S(2)}, u32[]{:S(2)}) collective-permute-start(f32[1,6,16,128]{3,2,1,0:T(8,128)S(1)} %maximum_bitcast_fusion.1), channel_id=1, source_target_pairs={{0,1},{1,2},{2,3},{3,4},{4,5},{5,6},{6,7},{8,9},{9,10},{10,11},{11... | collective-permute-start | bytes 147464 | tf_op jit(solution)/shard_map/ppermute | solution.py:19
  11.6 15.0 %all-to-all-start = ((s32[32,1,16]{2,1,0:T(1,128)}), s32[32,1,16]{2,1,0:T(1,128)S(1)}, u32[]{:S(2)}, u32[]{:S(2)}) async-start(s32[32,1,16]{2,1,0:T(1,128)} %bitcast.8), calls=%async_computation | async-start | bytes 32768 | tf_op jit(solution)/shard_map/all_to_all | solution.py:66
  26.6 63.5 %all-to-all-start.1 = ((bf16[32,16,1464]{2,1,0:T(8,128)(2,1)}), bf16[32,16,1464]{2,1,0:T(8,128)(2,1)S(1)}, u32[]{:S(2)}, u32[]{:S(2)}) async-start(bf16[32,16,1464]{2,1,0:T(8,128)(2,1)} %bitcast.9), calls=%async_computation.1 | async-start | bytes 3145728 | tf_op jit(solution)/shard_map/all_to_all | solution.py:65
  107.9 8.2 %copy-start = (bf16[1024,1464]{1,0:T(8,128)(2,1)S(1)}, bf16[1024,1464]{1,0:T(8,128)(2,1)}, u32[]{:S(2)}) copy-start(bf16[1024,1464]{1,0:T(8,128)(2,1)} %gather_fusion.1) | copy-start | bytes 8994820
where the time goes:
time: 127 us; the launch traced here: 125 us
  other arithmetic  41 us (32%)
  local copies, waits for them, and re-layouts  39.5 us (31%)
  matrix products  20.2 us (16%)
  starting transfers between devices  18.7 us (15%)
  waiting for transfers between devices  3.43 us (3%)
    dot_general x2, matrix products, on_device(): jnp.dot(picked, m2l_ops[direction], preferred_element_type=jnp.float32)  16.7 us
    reduce_sum x16, other arithmetic, leaf_velocity(): projected = jnp.sum(source_frc[:, :, None] * offset, axis=0)  16.4 us
    reduce_sum x16, other arithmetic, leaf_velocity(): return jnp.sum(summand, axis=1) * inv_eight_pi * target_live[None, :]  15.8 us
    dynamic_slice x32, local copies, waits for them, and re-layouts, leaves_block(): lax.map(one_leaf, (own_pos.transpose(1, 0, 2), own_live, leaf_lists.T))  11.6 us
    gather x2, local copies, waits for them, and re-layouts, on_device(): picked = multipoles[m2l_sources[0, direction]]  11.2 us
    gather x16, local copies, waits for them, and re-layouts, one_leaf(): chosen = source_table[:, leaf_list, :].reshape(6, -1)  8.88 us
    all_to_all x1, starting transfers between devices, on_device(): lax.all_to_all(slot_ids, 'hx', split_axis=0, concat_axis=0, tiled=True)  8.13 us
    ppermute x1, starting transfers between devices, padded(): before = lax.ppermute(last, axis, up)  4.99 us
  transfers between devices with their start and end apart: 4, of which 1 were waited for; matrix products, arithmetic and copies ran while one was open for 51% of the time, Pallas kernels for 0%

commit v1 on v0

v1 whole, which is shorter than its diff:
```python
import functools
import math

import jax
import jax.numpy as jnp
from jax import lax
from jax.experimental import pallas as pl
from jax.experimental.pallas import tpu as pltpu
from jax.sharding import PartitionSpec as P

EPS = 0.01
SCALE = 1.0 / (8.0 * math.pi)
MESH = pl.DeviceIdType.MESH
UNIQ = 4
CAP = 16
FEAT = 48
f32 = jnp.float32
bf16 = jnp.bfloat16
NT_DIMS = (((1,), (1,)), ((), ()))


def rounded(v):
    return v.astype(bf16).astype(f32)


def split3(v):
    a = rounded(v)
    b = rounded(v - a)
    return a, b, rounded(v - a - b)


def rank_keys(slots):
    lane = lax.broadcasted_iota(jnp.int32, slots.shape, 1)
    group = lax.broadcasted_iota(jnp.int32, slots.shape, 0)
    place = lane & (CAP - 1)
    dup = jnp.zeros(slots.shape, jnp.int32)
    for s in range(1, CAP):
        same = (pltpu.roll(slots, s, 1) == slots) & (place >= s)
        dup = jnp.where(same, 1, dup)
    first = (dup == 0) & (slots >= 0)
    named = jnp.where(first, slots, 1 << 20)
    rank = jnp.zeros(slots.shape, jnp.int32)
    for s in range(1, CAP):
        below = (pltpu.roll(named, s, 1) < slots) & (place >= s)
        rank = rank + jnp.where(below, 1, 0)
        below = (pltpu.roll(named, 128 - s, 1) < slots) & (place < CAP - s)
        rank = rank + jnp.where(below, 1, 0)
    key = jnp.where(slots >= 0, group * (128 // CAP * UNIQ) + (lane >> 4) * UNIQ + rank, -1)
    return key, first


def exchange_kernel(
    n_hx, n_nb, slots_ref, pos_ref, frc_ref, counts_ref, nbr_ref, rows_hbm, ops_hbm,
    prod_ref, ids_ref, vel_ref,
    rows, ops, send, recv, gathered, raw, ysrc, ylow, xtgt,
    send_sem, recv_sem, halo_send, halo_recv, rows_sem, ops_sem,
):
    hx, nb = lax.axis_index("hx"), lax.axis_index("nb")
    after, before = lax.rem(nb + 1, n_nb), lax.rem(nb + n_nb - 1, n_nb)
    coeffs = rows_hbm.shape[0]
    leaves, lanes = pos_ref.shape[1], pos_ref.shape[2]

    barrier = pltpu.get_barrier_semaphore()

    def greet(d, c):
        pl.semaphore_signal(barrier, inc=1, device_id={"hx": lax.rem(hx + d, n_hx)}, device_id_type=MESH)
        return c

    lax.fori_loop(1, n_hx, greet, 0)
    for other in (after, before):
        pl.semaphore_signal(barrier, inc=1, device_id={"nb": other}, device_id_type=MESH)

    rows_copy = pltpu.make_async_copy(rows_hbm, rows.at[pl.ds(0, coeffs), :], rows_sem)
    rows_copy.start()
    ops_copies = [pltpu.make_async_copy(ops_hbm.at[t], ops.at[t], ops_sem.at[t]) for t in range(ops.shape[0])]

    lane_ids = lax.broadcasted_iota(jnp.int32, (1, lanes), 1)
    for l in range(leaves):
        live = jnp.where(lane_ids < counts_ref[0, l], 1.0, 0.0).astype(f32)
        block = [pos_ref[c, l : l + 1, :] for c in range(3)]
        block += [frc_ref[c, l : l + 1, :] * live for c in range(3)]
        block += [jnp.ones((1, lanes), f32), jnp.zeros((1, lanes), f32)]
        raw[1, l] = jnp.concatenate(block, axis=0)

    slots = slots_ref[...]
    four = [slots[:, g * lanes : (g + 1) * lanes] for g in range(4)]
    slots8 = jnp.concatenate(four + four, axis=0)
    key, first = rank_keys(slots8)
    n_keys = n_hx * UNIQ
    key_ids = lax.broadcasted_iota(jnp.int32, (n_keys, lanes), 0)
    pick = jnp.concatenate(
        [jnp.where(key_ids == key[g : g + 1, :], 1.0, 0.0).astype(bf16) for g in range(4)], axis=1
    )
    high = jnp.where(first, slots8 >> 5, 0).astype(f32)
    low = jnp.where(first, slots8 & 31, 0).astype(f32)
    zero6 = jnp.zeros((6, lanes), f32)
    marks = jnp.concatenate(
        [jnp.concatenate([high[g : g + 1], low[g : g + 1], zero6], axis=0) for g in range(4)], axis=1
    )
    rows[coeffs : coeffs + 8, :] = marks.astype(bf16)
    rows_copy.wait()
    for c in ops_copies:
        c.start()
    sums = lax.dot_general(pick, rows[...], NT_DIMS, preferred_element_type=f32)
    for j in range(n_hx):
        send[j] = sums[j * UNIQ : (j + 1) * UNIQ, :].astype(bf16)

    pl.semaphore_wait(barrier, n_hx - 1 + 2)

    def halo(k, target):
        return pltpu.make_async_remote_copy(
            src_ref=raw.at[1], dst_ref=raw.at[k], send_sem=halo_send.at[k // 2], recv_sem=halo_recv.at[k // 2],
            device_id={"nb": target}, device_id_type=MESH,
        )

    up, down = halo(0, after), halo(2, before)
    up.start()
    down.start()

    def chunk(d):
        target = lax.rem(hx + d, n_hx)
        return pltpu.make_async_remote_copy(
            src_ref=send.at[target], dst_ref=recv.at[hx], send_sem=send_sem.at[d], recv_sem=recv_sem.at[d],
            device_id={"hx": target}, device_id_type=MESH,
        )

    def start(d, c):
        chunk(d).start()
        return c

    lax.fori_loop(1, n_hx, start, 0)
    recv[hx] = send[hx]

    row8 = lax.broadcasted_iota(jnp.int32, (leaves, 8, lanes), 1)
    own = raw[1]
    own_high = rounded(own)
    own_low = rounded(own - own_high)
    x_high, x_low = jnp.where(row8 < 3, own_high, 0.0), jnp.where(row8 < 3, own_low, 0.0)
    x_sum = x_high + x_low
    t1, t2, t3 = split3(jnp.sum(x_sum * x_sum, axis=1, keepdims=True) + EPS)
    is6 = row8 == 6
    zero8 = jnp.zeros((leaves, 8, lanes), f32)
    q_side = [
        jnp.where(is6, t1, -2.0 * x_high), -2.0 * x_high, jnp.where(is6, t2, -2.0 * x_low), -2.0 * x_low,
        jnp.where(is6, t3, jnp.where(row8 < 3, 1.0, 0.0)), zero8,
    ]
    force_rows = (row8 >= 3) & (row8 < 6)
    p_high, p_low = pltpu.roll(x_high, 3, 1), pltpu.roll(x_low, 3, 1)
    p_side = [p_high, p_high, p_low, p_low, jnp.where(force_rows, -1.0, 0.0), zero8]
    xtgt[:, :, :lanes] = jnp.concatenate(q_side, axis=1).astype(bf16)
    xtgt[:, :, lanes:] = jnp.concatenate(p_side, axis=1).astype(bf16)

    def source_side(k, mask):
        src = raw[k]
        if mask is not None:
            src = jnp.where(force_rows, src * mask, src)
        s_high = rounded(src)
        s_low = rounded(src - s_high)
        s_sum = s_high + s_low
        s_pos = jnp.where(row8 < 3, s_sum, 0.0)
        y1, y2, y3 = split3(jnp.sum(s_pos * s_pos, axis=1, keepdims=True))
        g1, g2, g3 = split3(jnp.sum(s_pos * pltpu.roll(s_sum, 5, 1), axis=1, keepdims=True))
        extra = zero8
        for at, v in enumerate((y1, y2, y3, g1, g2, g3, jnp.ones_like(y1))):
            extra = jnp.where(row8 == at, v, extra)
        table = jnp.concatenate([s_high, s_low, s_high, s_low, extra, zero8], axis=1)
        at = pl.ds(k * leaves, leaves)
        ysrc[at] = jnp.swapaxes(table, 1, 2).astype(bf16)
        ylow[at] = jnp.concatenate([s_high, s_low], axis=1).astype(bf16)

    source_side(1, None)
    up.wait_recv()
    source_side(0, jnp.where(nb > 0, 1.0, 0.0).astype(f32))
    down.wait_recv()
    source_side(2, jnp.where(nb < n_nb - 1, 1.0, 0.0).astype(f32))

    def leaf(i, c):
        x = xtgt[i]
        total = jnp.zeros((16, 2 * lanes), f32)
        for pair in range(nbr_ref.shape[0] // 2):
            kernels, weights = [], []
            for n in (2 * pair, 2 * pair + 1):
                which = nbr_ref[n, i]
                qp = jnp.dot(ysrc[which], x, preferred_element_type=f32)
                r = lax.rsqrt(qp[:, :lanes])
                w = r * r * r
                kernels.append(jnp.concatenate([r + EPS * w, qp[:, lanes:] * w], axis=1).astype(bf16))
                weights.append(ylow[which])
            total = total + jnp.dot(
                jnp.concatenate(weights, axis=1), jnp.concatenate(kernels, axis=0), preferred_element_type=f32
            )
        both = total[:8] + total[8:]
        first_part, second_part = both[:, :lanes], both[:, lanes:]
        x_own = raw[1, i]
        live = jnp.where(lane_ids < counts_ref[0, i], SCALE, 0.0).astype(f32)
        u = pltpu.roll(first_part, 5, 0) + x_own * second_part[6:7, :] - second_part
        vel_ref[i] = u * live
        return c

    lax.fori_loop(0, leaves, leaf, 0)

    def finish(d, c):
        chunk(d).wait_recv()
        return c

    lax.fori_loop(1, n_hx, finish, 0)
    for j in range(n_hx // 4):
        four = [recv[4 * j + k].astype(f32) for k in range(4)]
        gathered[16 * j : 16 * (j + 1), :] = jnp.concatenate(four, axis=0).astype(bf16)
    whose = gathered[:, coeffs : coeffs + 2].astype(f32)
    ids_ref[...] = jnp.broadcast_to((whose[:, 0:1] * 32.0 + whose[:, 1:2]).astype(jnp.int32), ids_ref.shape)
    for t, c in enumerate(ops_copies):
        c.wait()
        part = jnp.dot(gathered[:, :coeffs], ops[t], preferred_element_type=f32)
        prod_ref[t * n_keys : (t + 1) * n_keys, :] = part.astype(bf16)

    def sent(d, c):
        chunk(d).wait_send()
        return c

    lax.fori_loop(1, n_hx, sent, 0)
    up.wait_send()
    down.wait_send()


def select_kernel(ids_ref, src_ref, prod_ref, vel_in, out_ref, vel_out, prod_t):
    @pl.when(pl.program_id(0) == 0)
    def _():
        prod_t[...] = prod_ref[...].astype(f32).T.astype(bf16)
        v = vel_in[...]
        for c in range(3):
            vel_out[c] = v[:, c, :]

    ids = ids_ref[:, 0:1]
    pick = jnp.concatenate(
        [jnp.where(ids == src_ref[t : t + 1, :], 1.0, 0.0).astype(bf16) for t in range(src_ref.shape[0])], axis=0
    )
    out_ref[...] = jnp.dot(prod_t[...], pick, preferred_element_type=f32).astype(bf16)


def on_device(
    n_hx, n_nb, partial_multipoles, shared_slots, m2l_sources, m2l_ops, positions, forces, leaf_counts, neighbours
):
    rows_t = partial_multipoles[0].T
    coeffs, n_rows = rows_t.shape
    n_dirs, owned = m2l_sources.shape[1:]
    leaves = leaf_counts.shape[1]
    lanes = positions.shape[2] // leaves
    n_keys = n_hx * UNIQ
    vmem = pl.BlockSpec(memory_space=pltpu.VMEM)
    smem = pl.BlockSpec(memory_space=pltpu.SMEM)
    hbm = pl.BlockSpec(memory_space=pl.ANY)
    width = coeffs + 8
    prod, ids, vel = pl.pallas_call(
        functools.partial(exchange_kernel, n_hx, n_nb),
        out_shape=(
            jax.ShapeDtypeStruct((n_dirs * n_keys, coeffs), bf16),
            jax.ShapeDtypeStruct((n_keys, 128), jnp.int32),
            jax.ShapeDtypeStruct((leaves, 8, lanes), f32),
        ),
        in_specs=[vmem, vmem, vmem, smem, smem, hbm, hbm],
        out_specs=(vmem, vmem, vmem),
        scratch_shapes=[
            pltpu.VMEM((width, n_rows), bf16),
            pltpu.VMEM((n_dirs, coeffs, coeffs), bf16),
            pltpu.VMEM((n_hx, UNIQ, width), bf16),
            pltpu.VMEM((n_hx, UNIQ, width), bf16),
            pltpu.VMEM((n_keys, width), bf16),
            pltpu.VMEM((3, leaves, 8, lanes), f32),
            pltpu.VMEM((3 * leaves, lanes, FEAT), bf16),
            pltpu.VMEM((3 * leaves, 16, lanes), bf16),
            pltpu.VMEM((leaves, FEAT, 2 * lanes), bf16),
            pltpu.SemaphoreType.DMA((n_hx,)),
            pltpu.SemaphoreType.DMA((n_hx,)),
            pltpu.SemaphoreType.DMA((2,)),
            pltpu.SemaphoreType.DMA((2,)),
            pltpu.SemaphoreType.DMA,
            pltpu.SemaphoreType.DMA((n_dirs,)),
        ],
        compiler_params=pltpu.CompilerParams(
            collective_id=0, has_side_effects=True, vmem_limit_bytes=48 * 1024 * 1024
        ),
        name="exchange",
    )(
        shared_slots, positions.reshape(3, leaves, lanes), forces.reshape(3, leaves, lanes), leaf_counts,
        neighbours[0], rows_t, m2l_ops,
    )
    tile = 256
    out_t, velocity = pl.pallas_call(
        select_kernel,
        grid=(owned // tile,),
        out_shape=(
            jax.ShapeDtypeStruct((coeffs, owned), bf16),
            jax.ShapeDtypeStruct((3, leaves, lanes), f32),
        ),
        in_specs=[
            pl.BlockSpec((n_keys, 128), lambda i: (0, 0)),
            pl.BlockSpec((n_dirs, tile), lambda i: (0, i)),
            pl.BlockSpec((n_dirs * n_keys, coeffs), lambda i: (0, 0)),
            pl.BlockSpec((leaves, 8, lanes), lambda i: (0, 0, 0)),
        ],
        out_specs=(
            pl.BlockSpec((coeffs, tile), lambda i: (0, i)),
            pl.BlockSpec((3, leaves, lanes), lambda i: (0, 0, 0)),
        ),
        scratch_shapes=[pltpu.VMEM((coeffs, n_dirs * n_keys), bf16)],
        compiler_params=pltpu.CompilerParams(dimension_semantics=("arbitrary",)),
        name="select",
    )(ids, m2l_sources[0], prod, vel)
    return out_t.T[None], velocity.reshape(1, 3, leaves * lanes)


def solution(mesh):
    placed = (
        P("nb", "hx", None),
        P("nb", "hx"),
        P("nb", None, "hx"),
        P(),
        P("nb", None, "hx"),
        P("nb", None, "hx"),
        P("nb", "hx"),
        P("nb", None, "hx"),
    )
    return jax.shard_map(
        functools.partial(on_device, mesh.shape["hx"], mesh.shape["nb"]),
        mesh=mesh,
        in_specs=placed,
        out_specs=(P("nb", "hx", None), P("nb", None, "hx")),
        check_vma=False,
    )
```

time: 127 us -> 42.3 us (0.33); the launches traced: 125 us -> 42 us
  other arithmetic: 41 us -> 0 us
  Pallas kernels: 0 us -> 34.3 us
  local copies, waits for them, and re-layouts: 39.5 us -> 6.99 us
  matrix products: 20.2 us -> 0 us
  starting transfers between devices: 18.7 us -> 0 us
  waiting for transfers between devices: 3.43 us -> 0 us
    pallas_call x0 -> x2, Pallas kernels: none -> 34.3 us  [the longest x1 29.6 us: on_device(): pl.pallas_call(functools.partial(exchange_kernel, n_hx, n_nb), out_shape=...]
    reduce_sum x32 -> x0, other arithmetic: 32.2 us -> none  [the longest x16 16.4 us: leaf_velocity(): projected = jnp.sum(source_frc[:, :, None] * offset, axis=0)]
    dot_general x3 -> x0, matrix products: 20.2 us -> none  [the longest x2 16.7 us: on_device(): jnp.dot(picked, m2l_ops[direction], preferred_element_type=jnp.float32)]
    gather x18 -> x0, local copies, waits for them, and re-layouts: 20.1 us -> none  [the longest x2 11.2 us: on_device(): picked = multipoles[m2l_sources[0, direction]]]
    all_to_all x2 -> x0, starting transfers between devices: 12.4 us -> none  [the longest x1 8.13 us: on_device(): lax.all_to_all(slot_ids, 'hx', split_axis=0, concat_axis=0, tiled=True)]
    dynamic_slice x32 -> x0, local copies, waits for them, and re-layouts: 11.6 us -> none  [leaves_block(): lax.map(one_leaf, (own_pos.transpose(1, 0, 2), own_live, leaf_lists.T))]
    ppermute x2 -> x0, starting transfers between devices: 6.27 us -> none  [the longest x1 4.99 us: padded(): before = lax.ppermute(last, axis, up)]
    unnamed x6 -> x18, local copies, waits for them, and re-layouts: 3.08 us -> 6.99 us
  transfers between devices with their start and end apart: 4 -> 0, of which waited for: 1 -> 0; matrix products, arithmetic and copies ran while one was open for 51% -> 0% of each run, Pallas kernels for 0% -> 0%
where the time goes in v1:
time: 42.3 us; the launch traced here: 42 us
  Pallas kernels  34.3 us (81%)
  local copies, waits for them, and re-layouts  6.99 us (17%)
  between operations  0.66 us (2%)
    pallas_call x1, Pallas kernels, on_device(): pl.pallas_call(functools.partial(exchange_kernel, n_hx, n_nb), out_shape=...  29.6 us
    unnamed x18, local copies, waits for them, and re-layouts  6.99 us
    pallas_call x1, Pallas kernels, on_device(): pl.pallas_call(select_kernel, grid=(owned // tile,), out_shape=(jax.Shape...  4.7 us

profile of v1, /device:TPU:1, one launch (start us, length us, event | category | flops | bytes accessed | tf_op | source)
XLA Modules:
  0.0 42.0 jit_solution(11382092811514729543)
XLA Ops:
  0.6 0.0 copy-start
  0.6 1.4 %copy-done = bf16[1,512,1464]{1,2,0:T(8,128)(2,1)S(1)} copy-done((bf16[1,512,1464]{1,2,0:T(8,128)(2,1)S(1)}, bf16[1,512,1464]{1,2,0:T(8,128)(2,1)}, u32[]{:S(2)}) %copy-start) | copy-done | bytes 1499160
  2.0 0.0 copy-start.4
  2.0 0.7 %copy-done.4 = f32[1,3,2048]{2,0,1:T(1,128)S(1)} copy-done((f32[1,3,2048]{2,0,1:T(1,128)S(1)}, f32[1,3,2048]{2,0,1:T(1,128)}, u32[]{:S(2)}) %copy-start.4) | copy-done | bytes 24600
  2.8 0.0 copy-start.5
  2.8 0.7 %copy-done.5 = f32[1,3,2048]{2,0,1:T(1,128)S(1)} copy-done((f32[1,3,2048]{2,0,1:T(1,128)S(1)}, f32[1,3,2048]{2,0,1:T(1,128)}, u32[]{:S(2)}) %copy-start.5) | copy-done | bytes 24600
  3.5 0.0 copy-start.6
  3.5 0.7 %copy-done.6 = s32[1,8,16]{2,1,0:T(8,128)S(1)} copy-done((s32[1,8,16]{2,1,0:T(8,128)S(1)}, s32[1,8,16]{2,1,0:T(8,128)}, u32[]{:S(2)}) %copy-start.6) | copy-done | bytes 536
  4.2 0.0 copy-start.7
  4.2 0.7 %copy-done.7 = s32[1,512]{1,0:T(1,128)S(1)} copy-done((s32[1,512]{1,0:T(1,128)S(1)}, s32[1,512]{1,0:T(1,128)}, u32[]{:S(2)}) %copy-start.7) | copy-done | bytes 2072
  4.9 0.0 copy-start.8
  4.9 0.7 %copy-done.8 = s32[1,16]{1,0:T(1,128)S(1)} copy-done((s32[1,16]{1,0:T(1,128)S(1)}, s32[1,16]{1,0:T(1,128)}, u32[]{:S(2)}) %copy-start.8) | copy-done | bytes 88
  5.5 29.6 %exchange.1 = (bf16[256,1464]{1,0:T(8,128)(2,1)S(1)}, s32[128,128]{1,0:T(8,128)S(1)}, f32[16,8,128]{2,1,0:T(8,128)S(1)}) custom-call(s32[1,512]{1,0:T(1,128)S(1)} %copy-done.7, f32[3,16,128]{2,1,0:T(8,128)S(1)} %bitcast.12, f32[3,16,128]{2,1,0:T(8,128)S(1)} %bitcast.13, s32[1,16]{1,0:T(1,128)S(1)} %copy-done.8, s32[8,16]{1,0:T(8,128)S(1)} %bitcast.14, ...), custom_call_target="tpu_custom_call" | custom-call | tf_op jit(solution)/shard_map/exchange/pallas_call | solution.py:254
  35.2 0.0 copy-start.1
  35.2 0.9 %copy-done.1 = bf16[256,1464]{1,0:T(8,128)(2,1)} copy-done((bf16[256,1464]{1,0:T(8,128)(2,1)}, bf16[256,1464]{1,0:T(8,128)(2,1)S(1)}, u32[]{:S(2)}) %copy-start.1) | copy-done | bytes 749592
  36.0 0.0 copy-start.2
  36.0 0.6 %copy-done.2 = s32[128,128]{1,0:T(8,128)} copy-done((s32[128,128]{1,0:T(8,128)}, s32[128,128]{1,0:T(8,128)S(1)}, u32[]{:S(2)}) %copy-start.2) | copy-done | bytes 65560
  36.7 0.0 copy-start.3
  36.7 0.6 %copy-done.3 = f32[16,8,128]{2,1,0:T(8,128)} copy-done((f32[16,8,128]{2,1,0:T(8,128)}, f32[16,8,128]{2,1,0:T(8,128)S(1)}, u32[]{:S(2)}) %copy-start.3) | copy-done | bytes 65560
  37.3 4.7 %select.1 = (bf16[1464,1024]{1,0:T(8,128)(2,1)}, f32[3,16,128]{2,1,0:T(8,128)}) custom-call(s32[128,128]{1,0:T(8,128)} %copy-done.2, s32[2,1024]{1,0:T(2,128)} %bitcast.15, bf16[256,1464]{1,0:T(8,128)(2,1)} %copy-done.1, f32[16,8,128]{2,1,0:T(8,128)} %copy-done.3), custom_call_target="tpu_custom_call" | custom-call | tf_op jit(solution)/shard_map/select/pallas_call | solution.py:289
Async XLA Ops:
  0.6 1.4 %copy-start = (bf16[1,512,1464]{1,2,0:T(8,128)(2,1)S(1)}, bf16[1,512,1464]{1,2,0:T(8,128)(2,1)}, u32[]{:S(2)}) copy-start(bf16[1,512,1464]{1,2,0:T(8,128)(2,1)} %param.8) | copy-start | bytes 4497412
  2.0 0.7 %copy-start.4 = (f32[1,3,2048]{2,0,1:T(1,128)S(1)}, f32[1,3,2048]{2,0,1:T(1,128)}, u32[]{:S(2)}) copy-start(f32[1,3,2048]{2,0,1:T(1,128)} %param.12) | copy-start | bytes 73732
  2.8 0.7 %copy-start.5 = (f32[1,3,2048]{2,0,1:T(1,128)S(1)}, f32[1,3,2048]{2,0,1:T(1,128)}, u32[]{:S(2)}) copy-start(f32[1,3,2048]{2,0,1:T(1,128)} %param.13) | copy-start | bytes 73732
  3.5 0.7 %copy-start.6 = (s32[1,8,16]{2,1,0:T(8,128)S(1)}, s32[1,8,16]{2,1,0:T(8,128)}, u32[]{:S(2)}) copy-start(s32[1,8,16]{2,1,0:T(8,128)} %param.15) | copy-start | bytes 1540
  4.2 0.7 %copy-start.7 = (s32[1,512]{1,0:T(1,128)S(1)}, s32[1,512]{1,0:T(1,128)}, u32[]{:S(2)}) copy-start(s32[1,512]{1,0:T(1,128)} %slots_ref.1) | copy-start | bytes 6148
  4.9 0.7 %copy-start.8 = (s32[1,16]{1,0:T(1,128)S(1)}, s32[1,16]{1,0:T(1,128)}, u32[]{:S(2)}) copy-start(s32[1,16]{1,0:T(1,128)} %counts_ref.1) | copy-start | bytes 196
  35.2 0.9 %copy-start.1 = (bf16[256,1464]{1,0:T(8,128)(2,1)}, bf16[256,1464]{1,0:T(8,128)(2,1)S(1)}, u32[]{:S(2)}) copy-start(bf16[256,1464]{1,0:T(8,128)(2,1)S(1)} %get-tuple-element.8.prod_ref) | copy-start | bytes 2248708
  36.0 0.6 %copy-start.2 = (s32[128,128]{1,0:T(8,128)}, s32[128,128]{1,0:T(8,128)S(1)}, u32[]{:S(2)}) copy-start(s32[128,128]{1,0:T(8,128)S(1)} %get-tuple-element.7.ids_ref) | copy-start | bytes 196612
  36.7 0.6 %copy-start.3 = (f32[16,8,128]{2,1,0:T(8,128)}, f32[16,8,128]{2,1,0:T(8,128)S(1)}, u32[]{:S(2)}) copy-start(f32[16,8,128]{2,1,0:T(8,128)S(1)} %get-tuple-element.9.vel_in) | copy-start | bytes 196612

commit v2 on v1

v2 whole, which is shorter than its diff:
```python
import functools
import math

import jax
import jax.numpy as jnp
from jax import lax
from jax.experimental import pallas as pl
from jax.experimental.pallas import tpu as pltpu
from jax.sharding import PartitionSpec as P

EPS = 0.01
SCALE = 1.0 / (8.0 * math.pi)
MESH = pl.DeviceIdType.MESH
UNIQ = 4
CAP = 16
QROWS = 32
FROWS = 48
f32 = jnp.float32
bf16 = jnp.bfloat16
NT_DIMS = (((1,), (1,)), ((), ()))


def rounded(v):
    return v.astype(bf16).astype(f32)


def split3(v):
    a = rounded(v)
    b = rounded(v - a)
    return a, b, rounded(v - a - b)


def rank_keys(slots):
    lane = lax.broadcasted_iota(jnp.int32, slots.shape, 1)
    group = lax.broadcasted_iota(jnp.int32, slots.shape, 0)
    place = lane & (CAP - 1)
    dup = jnp.zeros(slots.shape, jnp.int32)
    for s in range(1, CAP):
        same = (pltpu.roll(slots, s, 1) == slots) & (place >= s)
        dup = jnp.where(same, 1, dup)
    first = (dup == 0) & (slots >= 0)
    named = jnp.where(first, slots, 1 << 20)
    rank = jnp.zeros(slots.shape, jnp.int32)
    for s in range(1, CAP):
        below = (pltpu.roll(named, s, 1) < slots) & (place >= s)
        rank = rank + jnp.where(below, 1, 0)
        below = (pltpu.roll(named, 128 - s, 1) < slots) & (place < CAP - s)
        rank = rank + jnp.where(below, 1, 0)
    key = jnp.where(slots >= 0, group * (128 // CAP * UNIQ) + (lane >> 4) * UNIQ + rank, -1)
    return key, first


def exchange_kernel(
    n_hx, n_nb, slots_hbm, pos_hbm, frc_hbm, counts_hbm, nbr_hbm, src_hbm, rows_hbm, ops_hbm,
    prod_ref, pick_ref, vel_ref,
    slots_ref, pos_ref, frc_ref, counts_ref, nbr_ref, src_ref,
    rows, ops, send, recv, gathered, raw, alive, yq, feat, xtgt, moments,
    send_sem, recv_sem, halo_send, halo_recv, small_sem, rows_sem, ops_sem,
):
    hx, nb = lax.axis_index("hx"), lax.axis_index("nb")
    after, before = lax.rem(nb + 1, n_nb), lax.rem(nb + n_nb - 1, n_nb)
    coeffs = rows_hbm.shape[0]
    leaves, lanes = pos_ref.shape[1], pos_ref.shape[2]
    half = send.shape[2]
    n_keys = n_hx * UNIQ

    small = [
        pltpu.make_async_copy(a, b, small_sem.at[k])
        for k, (a, b) in enumerate(
            (
                (slots_hbm, slots_ref), (counts_hbm, counts_ref), (pos_hbm, pos_ref), (frc_hbm, frc_ref),
                (nbr_hbm, nbr_ref), (src_hbm, src_ref),
            )
        )
    ]
    for c in small[:4]:
        c.start()
    rows_copy = pltpu.make_async_copy(rows_hbm, rows.at[pl.ds(0, coeffs), :], rows_sem)
    rows_copy.start()
    for c in small[4:]:
        c.start()

    barrier = pltpu.get_barrier_semaphore()
    for d in range(1, n_hx):
        pl.semaphore_signal(barrier, inc=1, device_id={"hx": lax.rem(hx + d, n_hx)}, device_id_type=MESH)
    for other in (after, before):
        pl.semaphore_signal(barrier, inc=1, device_id={"nb": other}, device_id_type=MESH)

    ops_copies = [pltpu.make_async_copy(ops_hbm.at[t], ops.at[t], ops_sem.at[t]) for t in range(ops.shape[0])]

    small[0].wait()
    slots = slots_ref[...]
    four = [slots[:, g * lanes : (g + 1) * lanes] for g in range(4)]
    slots8 = jnp.concatenate(four + four, axis=0)
    key, first = rank_keys(slots8)
    key_ids = lax.broadcasted_iota(jnp.int32, (n_keys, lanes), 0)
    choose = jnp.concatenate(
        [jnp.where(key_ids == key[g : g + 1, :], 1.0, 0.0).astype(bf16) for g in range(4)], axis=1
    )
    high = jnp.where(first, slots8 >> 5, 0).astype(f32)
    low = jnp.where(first, slots8 & 31, 0).astype(f32)
    zero6 = jnp.zeros((6, lanes), f32)
    marks = jnp.concatenate(
        [jnp.concatenate([high[g : g + 1], low[g : g + 1], zero6], axis=0) for g in range(4)], axis=1
    )
    rows[coeffs : coeffs + 8, :] = marks.astype(bf16)
    rows[coeffs + 8 :, :] = jnp.zeros((rows.shape[0] - coeffs - 8, rows.shape[1]), bf16)

    for c in small[1:4]:
        c.wait()
    lane_ids = lax.broadcasted_iota(jnp.int32, (1, lanes), 1)
    for l in range(leaves):
        live = jnp.where(lane_ids < counts_ref[0, l], 1.0, 0.0).astype(f32)
        alive[l : l + 1, :] = live
        block = [pos_ref[c, l : l + 1, :] for c in range(3)]
        block += [frc_ref[c, l : l + 1, :] * live for c in range(3)]
        block += [jnp.ones((1, lanes), f32), jnp.zeros((1, lanes), f32)]
        raw[1, l] = jnp.concatenate(block, axis=0)

    rows_copy.wait()
    for c in ops_copies:
        c.start()
    sums = lax.dot_general(choose, rows[...], NT_DIMS, preferred_element_type=f32)
    upper = lax.broadcasted_iota(jnp.int32, (8, half), 0) < UNIQ
    for v in range(n_hx // 2):
        left, right = sums[8 * v : 8 * v + 8, :half], sums[8 * v : 8 * v + 8, half:]
        send[2 * v] = jnp.where(upper, left, pltpu.roll(right, UNIQ, 0)).astype(bf16)
        send[2 * v + 1] = jnp.where(upper, pltpu.roll(left, UNIQ, 0), right).astype(bf16)

    pl.semaphore_wait(barrier, n_hx - 1 + 2)

    def halo(k, target):
        return pltpu.make_async_remote_copy(
            src_ref=raw.at[1], dst_ref=raw.at[k], send_sem=halo_send.at[k // 2], recv_sem=halo_recv.at[k // 2],
            device_id={"nb": target}, device_id_type=MESH,
        )

    up, down = halo(0, after), halo(2, before)
    up.start()
    down.start()

    def chunk(d):
        target = lax.rem(hx + d, n_hx)
        return pltpu.make_async_remote_copy(
            src_ref=send.at[target], dst_ref=recv.at[hx], send_sem=send_sem.at[d], recv_sem=recv_sem.at[d],
            device_id={"hx": target}, device_id_type=MESH,
        )

    chunks = [chunk(d) for d in range(1, n_hx)]
    for c in chunks:
        c.start()
    recv[hx] = send[hx]

    row8 = lax.broadcasted_iota(jnp.int32, (leaves, 8, lanes), 1)
    zero8 = jnp.zeros((leaves, 8, lanes), f32)
    is_pos, is_frc = row8 < 3, (row8 >= 3) & (row8 < 6)

    def pos_sum(v):
        return jnp.sum(jnp.where(is_pos, v, 0.0), axis=1, keepdims=True)

    own = raw[1]
    own_high = rounded(own)
    own_low = rounded(own - own_high)
    x_sum = own_high + own_low
    t1, t2, t3 = split3(pos_sum(x_sum * x_sum) + EPS)
    two_high, two_low = -2.0 * own_high, -2.0 * own_low
    x_table = jnp.concatenate(
        [
            jnp.where(is_pos, two_high, jnp.where(is_frc, pltpu.roll(two_high, 3, 1), jnp.where(row8 == 6, t1, t2))),
            jnp.where(is_pos, two_low, jnp.where(is_frc, pltpu.roll(two_low, 3, 1), jnp.where(row8 == 6, t3, 0.0))),
            jnp.where(is_pos, 1.0, zero8),
            zero8,
        ],
        axis=1,
    )
    xtgt[...] = jnp.swapaxes(x_table, 1, 2).astype(bf16)

    def source_side(k, mask):
        src = raw[k]
        if mask is not None:
            src = jnp.where(is_frc, src * mask, src)
        at = pl.ds(k * leaves, leaves)
        s_high = rounded(src)
        s_low = rounded(src - s_high)
        s_sum = s_high + s_low
        y1, y2, y3 = split3(pos_sum(s_sum * s_sum))
        pairs = jnp.where(is_pos, s_high, jnp.where(is_frc, pltpu.roll(s_low, 3, 1), 1.0))
        squares = jnp.where(row8 == 0, y1, jnp.where(row8 == 1, y2, jnp.where(row8 == 2, y3, 0.0)))
        yq[at] = jnp.concatenate([pairs, pairs, squares, zero8], axis=1).astype(bf16)
        square = pos_sum(src * src)
        f_at0, f_at6 = pltpu.roll(src, 5, 1), pltpu.roll(src, 3, 1)
        f_dot_y = pos_sum(src * f_at0)
        z = src[:, 2:3, :]
        products = jnp.where(is_pos, f_at0, jnp.where(is_frc, src, f_at6)) * jnp.where(
            is_pos, src[:, 0:1, :], jnp.where(is_frc, src[:, 1:2, :], z)
        )
        second = pltpu.roll(src, 1, 1) * square + pltpu.roll(src, 4, 1) * f_dot_y
        others = jnp.where(
            row8 == 0, f_at6 * z, jnp.where(row8 < 4, pltpu.roll(src, 6, 1), jnp.where(row8 < 7, second, 0.0))
        )
        a, b = split3(products), split3(others)
        feat[at] = jnp.concatenate([a[0], b[0], a[1], b[1], a[2], b[2]], axis=1).astype(bf16)

    source_side(1, None)
    up.wait_recv()
    source_side(0, jnp.where(nb > 0, 1.0, 0.0).astype(f32))
    down.wait_recv()
    source_side(2, jnp.where(nb < n_nb - 1, 1.0, 0.0).astype(f32))
    small[4].wait()

    def leaf(i, c):
        which = [nbr_ref[n, i] for n in range(nbr_ref.shape[0])]
        q = jnp.dot(xtgt[i], jnp.concatenate([yq[n] for n in which], axis=1), preferred_element_type=f32)
        r = lax.rsqrt(q)
        w = (r * r * r).astype(bf16)
        m = lax.dot_general(
            jnp.concatenate([feat[n] for n in which], axis=1), w, NT_DIMS, preferred_element_type=f32
        )
        moments[i] = m[:16] + m[16:32] + m[32:]
        return c

    lax.fori_loop(0, leaves, leaf, 0, unroll=True)
    m = [moments[:, k, :] for k in range(15)]
    x = [pos_ref[c] for c in range(3)]
    two_e = x[0] * x[0] + x[1] * x[1] + x[2] * x[2] + 2.0 * EPS
    along = x[0] * m[9] + x[1] * m[10] + x[2] * m[11] - (m[0] + m[4] + m[8])
    live = alive[...] * SCALE
    for c in range(3):
        u = two_e * m[9 + c] + x[c] * along + m[12 + c]
        for b in range(3):
            u = u - x[b] * (2.0 * m[3 * b + c] + m[3 * c + b])
        vel_ref[c] = u * live

    for c in chunks:
        c.wait_recv()
    for v in range(n_hx // 4):
        lefts, rights = [], []
        for k in (4 * v, 4 * v + 2):
            a, b = recv[k].astype(f32), recv[k + 1].astype(f32)
            lefts.append(jnp.where(upper, a, pltpu.roll(b, UNIQ, 0)))
            rights.append(jnp.where(upper, pltpu.roll(a, UNIQ, 0), b))
        gathered[16 * v : 16 * (v + 1), :half] = jnp.concatenate(lefts, axis=0).astype(bf16)
        gathered[16 * v : 16 * (v + 1), half:] = jnp.concatenate(rights, axis=0).astype(bf16)
    whose = gathered[:, coeffs : coeffs + 2].astype(f32)
    ids = (whose[:, 0:1] * 32.0 + whose[:, 1:2]).astype(jnp.int32)
    small[5].wait()
    for t, c in enumerate(ops_copies):
        c.wait()
        part = jnp.dot(gathered[:, :coeffs], ops[t], preferred_element_type=f32)
        prod_ref[:, t * n_keys : (t + 1) * n_keys] = part.T.astype(bf16)
        pick_ref[t * n_keys : (t + 1) * n_keys, :] = jnp.where(ids == src_ref[t : t + 1, :], 1.0, 0.0).astype(bf16)

    for c in chunks:
        c.wait_send()
    up.wait_send()
    down.wait_send()


def select_kernel(prod_ref, pick_ref, vel_in, out_ref, vel_out):
    @pl.when(pl.program_id(0) == 0)
    def _():
        vel_out[...] = vel_in[...]

    at = pl.ds(pl.multiple_of(pl.program_id(0) * out_ref.shape[1], 128), out_ref.shape[1])
    out_ref[...] = jnp.dot(prod_ref[...], pick_ref[:, at], preferred_element_type=f32).astype(bf16)


def on_device(
    n_hx, n_nb, partial_multipoles, shared_slots, m2l_sources, m2l_ops, positions, forces, leaf_counts, neighbours
):
    rows_t = partial_multipoles[0].T
    coeffs, n_rows = rows_t.shape
    n_dirs, owned = m2l_sources.shape[1:]
    n_near = neighbours.shape[1]
    leaves = leaf_counts.shape[1]
    lanes = positions.shape[2] // leaves
    n_keys = n_hx * UNIQ
    vmem = pl.BlockSpec(memory_space=pltpu.VMEM)
    hbm = pl.BlockSpec(memory_space=pltpu.HBM)
    half = pl.cdiv(coeffs + 8, 256) * 128
    i32 = jnp.int32
    prod, pick, vel = pl.pallas_call(
        functools.partial(exchange_kernel, n_hx, n_nb),
        out_shape=(
            jax.ShapeDtypeStruct((coeffs, n_dirs * n_keys), bf16),
            jax.ShapeDtypeStruct((n_dirs * n_keys, owned), bf16),
            jax.ShapeDtypeStruct((3, leaves, lanes), f32),
        ),
        in_specs=[hbm] * 8,
        out_specs=(vmem, vmem, vmem),
        scratch_shapes=[
            pltpu.VMEM((1, n_rows), i32),
            pltpu.VMEM((3, leaves, lanes), f32),
            pltpu.VMEM((3, leaves, lanes), f32),
            pltpu.SMEM((1, leaves), i32),
            pltpu.SMEM((n_near, leaves), i32),
            pltpu.VMEM((n_dirs, owned), i32),
            pltpu.VMEM((2 * half, n_rows), bf16),
            pltpu.VMEM((n_dirs, coeffs, coeffs), bf16),
            pltpu.VMEM((n_hx, 2 * UNIQ, half), bf16),
            pltpu.VMEM((n_hx, 2 * UNIQ, half), bf16),
            pltpu.VMEM((n_keys, 2 * half), bf16),
            pltpu.VMEM((3, leaves, 8, lanes), f32),
            pltpu.VMEM((leaves, lanes), f32),
            pltpu.VMEM((3 * leaves, QROWS, lanes), bf16),
            pltpu.VMEM((3 * leaves, FROWS, lanes), bf16),
            pltpu.VMEM((leaves, lanes, QROWS), bf16),
            pltpu.VMEM((leaves, 16, lanes), f32),
            pltpu.SemaphoreType.DMA((n_hx,)),
            pltpu.SemaphoreType.DMA((n_hx,)),
            pltpu.SemaphoreType.DMA((2,)),
            pltpu.SemaphoreType.DMA((2,)),
            pltpu.SemaphoreType.DMA((6,)),
            pltpu.SemaphoreType.DMA,
            pltpu.SemaphoreType.DMA((n_dirs,)),
        ],
        compiler_params=pltpu.CompilerParams(
            collective_id=0, has_side_effects=True, vmem_limit_bytes=48 * 1024 * 1024
        ),
        name="exchange",
    )(
        *[
            pltpu.with_memory_space_constraint(v, pltpu.HBM)
            for v in (
                shared_slots, positions.reshape(3, leaves, lanes), forces.reshape(3, leaves, lanes), leaf_counts,
                neighbours[0], m2l_sources[0], rows_t, m2l_ops,
            )
        ]
    )
    tile = 256
    out_t, velocity = pl.pallas_call(
        select_kernel,
        grid=(owned // tile,),
        out_shape=(
            jax.ShapeDtypeStruct((coeffs, owned), bf16),
            jax.ShapeDtypeStruct((3, leaves, lanes), f32),
        ),
        in_specs=[vmem, vmem, vmem],
        out_specs=(
            pl.BlockSpec((coeffs, tile), lambda i: (0, i)),
            pl.BlockSpec((3, leaves, lanes), lambda i: (0, 0, 0)),
        ),
        compiler_params=pltpu.CompilerParams(dimension_semantics=("arbitrary",), vmem_limit_bytes=16 * 1024 * 1024),
        name="select",
    )(prod, pick, vel)
    return out_t.T[None], velocity.reshape(1, 3, leaves * lanes)


def solution(mesh):
    placed = (
        P("nb", "hx", None),
        P("nb", "hx"),
        P("nb", None, "hx"),
        P(),
        P("nb", None, "hx"),
        P("nb", None, "hx"),
        P("nb", "hx"),
        P("nb", None, "hx"),
    )
    return jax.shard_map(
        functools.partial(on_device, mesh.shape["hx"], mesh.shape["nb"]),
        mesh=mesh,
        in_specs=placed,
        out_specs=(P("nb", "hx", None), P("nb", None, "hx")),
        check_vma=False,
    )
```

time: 42.3 us -> 24 us (0.57)
  Pallas kernels: 34.3 us -> 23.2 us
  local copies, waits for them, and re-layouts: 6.99 us -> 0 us
    pallas_call x1, Pallas kernels: 29.6 us -> 20.3 us  [on_device(): pl.pallas_call(functools.partial(exchange_kernel, n_hx, n_nb), out_shape=...]
    unnamed x18 -> x0, local copies, waits for them, and re-layouts: 6.99 us -> none
    pallas_call x1, Pallas kernels: 4.7 us -> 2.89 us  [on_device(): pl.pallas_call(select_kernel, grid=(owned // tile,), out_shape=(jax.Shape...]
where the time goes in v2:
time: 24 us; the launch traced here: 23.9 us
  Pallas kernels  23.2 us (97%)
  between operations  0.64 us (3%)
    pallas_call x1, Pallas kernels, on_device(): pl.pallas_call(functools.partial(exchange_kernel, n_hx, n_nb), out_shape=...  20.3 us
    pallas_call x1, Pallas kernels, on_device(): pl.pallas_call(select_kernel, grid=(owned // tile,), out_shape=(jax.Shape...  2.89 us

profile of v2, /device:TPU:1, one launch (start us, length us, event | category | flops | bytes accessed | tf_op | source)
XLA Modules:
  0.0 23.9 jit_solution(12749923686454377069)
XLA Ops:
  0.6 20.3 %exchange.1 = (bf16[1464,256]{1,0:T(8,128)(2,1)S(1)}, bf16[256,1024]{1,0:T(8,128)(2,1)S(1)}, f32[3,16,128]{2,1,0:T(8,128)S(1)}) custom-call(s32[1,512]{1,0:T(1,128)} %slots_hbm.1, f32[3,16,128]{2,1,0:T(8,128)} %bitcast.12, f32[3,16,128]{2,1,0:T(8,128)} %bitcast.13, s32[1,16]{1,0:T(1,128)} %counts_hbm.1, s32[8,16]{1,0:T(8,128)} %bitcast.15, ...), custom_call_target="tpu_custom_call" | custom-call | tf_op jit(solution)/shard_map/exchange/pallas_call | solution.py:282
  21.0 2.9 %select.1 = (bf16[1464,1024]{1,0:T(8,128)(2,1)}, f32[3,16,128]{2,1,0:T(8,128)}) custom-call(bf16[1464,256]{1,0:T(8,128)(2,1)S(1)} %get-tuple-element.7.prod_ref, bf16[256,1024]{1,0:T(8,128)(2,1)S(1)} %get-tuple-element.8.pick_ref, f32[3,16,128]{2,1,0:T(8,128)S(1)} %get-tuple-element.9.vel_in), custom_call_target="tpu_custom_call" | custom-call | tf_op jit(solution)/shard_map/select/pallas_call | solution.py:331

commit v3 on v2

--- a/solution.py
+++ b/solution.py
@@ -18,6 +18,12 @@
 f32 = jnp.float32
 bf16 = jnp.bfloat16
 NT_DIMS = (((1,), (1,)), ((), ()))
+
+
+def peer_steps(n_hx):
+    side = math.isqrt(n_hx // 2)
+    steps = [(dx, dy, dc) for dx in range(side) for dy in range(side) for dc in range(2) if dx or dy or dc]
+    return side, sorted(steps, key=lambda s: -(min(s[0], side - s[0]) + min(s[1], side - s[1])))
 
 
 def rounded(v):
@@ -80,9 +86,15 @@
     for c in small[4:]:
         c.start()
 
+    side, steps = peer_steps(n_hx)
+    at_x, at_y, at_c = hx // (2 * side), lax.rem(hx // 2, side), lax.rem(hx, 2)
+
+    def peer(dx, dy, dc):
+        return lax.rem(at_x + dx, side) * (2 * side) + lax.rem(at_y + dy, side) * 2 + lax.rem(at_c + dc, 2)
+
     barrier = pltpu.get_barrier_semaphore()
-    for d in range(1, n_hx):
-        pl.semaphore_signal(barrier, inc=1, device_id={"hx": lax.rem(hx + d, n_hx)}, device_id_type=MESH)
+    for step in steps:
+        pl.semaphore_signal(barrier, inc=1, device_id={"hx": peer(*step)}, device_id_type=MESH)
     for other in (after, before):
         pl.semaphore_signal(barrier, inc=1, device_id={"nb": other}, device_id_type=MESH)
 
@@ -139,14 +151,14 @@
     up.start()
     down.start()
 
-    def chunk(d):
-        target = lax.rem(hx + d, n_hx)
+    def chunk(d, step):
+        target = peer(*step)
         return pltpu.make_async_remote_copy(
             src_ref=send.at[target], dst_ref=recv.at[hx], send_sem=send_sem.at[d], recv_sem=recv_sem.at[d],
             device_id={"hx": target}, device_id_type=MESH,
         )
 
-    chunks = [chunk(d) for d in range(1, n_hx)]
+    chunks = [chunk(d, step) for d, step in enumerate(steps)]
     for c in chunks:
         c.start()
     recv[hx] = send[hx]
@@ -244,8 +256,9 @@
     whose = gathered[:, coeffs : coeffs + 2].astype(f32)
     ids = (whose[:, 0:1] * 32.0 + whose[:, 1:2]).astype(jnp.int32)
     small[5].wait()
-    for t, c in enumerate(ops_copies):
+    for c in ops_copies:
         c.wait()
+    for t in range(ops.shape[0]):
         part = jnp.dot(gathered[:, :coeffs], ops[t], preferred_element_type=f32)
         prod_ref[:, t * n_keys : (t + 1) * n_keys] = part.T.astype(bf16)
         pick_ref[t * n_keys : (t + 1) * n_keys, :] = jnp.where(ids == src_ref[t : t + 1, :], 1.0, 0.0).astype(bf16)
@@ -256,13 +269,17 @@
     down.wait_send()
 
 
-def select_kernel(prod_ref, pick_ref, vel_in, out_ref, vel_out):
-    @pl.when(pl.program_id(0) == 0)
-    def _():
-        vel_out[...] = vel_in[...]
-
-    at = pl.ds(pl.multiple_of(pl.program_id(0) * out_ref.shape[1], 128), out_ref.shape[1])
-    out_ref[...] = jnp.dot(prod_ref[...], pick_ref[:, at], preferred_element_type=f32).astype(bf16)
+def select_kernel(parts, prod_ref, pick_ref, vel_in, out_hbm, vel_out, buffer, sems):
+    vel_out[...] = vel_in[...]
+    copies, at = [], 0
+    for k, size in enumerate(parts):
+        rows = slice(at, at + size)
+        buffer[rows, :] = jnp.dot(prod_ref[rows, :], pick_ref[...], preferred_element_type=f32).astype(bf16)
+        copies.append(pltpu.make_async_copy(buffer.at[pl.ds(at, size)], out_hbm.at[pl.ds(at, size)], sems.at[k]))
+        copies[-1].start()
+        at += size
+    for c in copies:
+        c.wait()
 
 
 def on_device(
@@ -327,20 +344,18 @@
             )
         ]
     )
-    tile = 256
+    step = pl.cdiv(coeffs, 8 * 8) * 8
+    parts = [min(step, coeffs - k) for k in range(0, coeffs, step)]
     out_t, velocity = pl.pallas_call(
-        select_kernel,
-        grid=(owned // tile,),
+        functools.partial(select_kernel, parts),
         out_shape=(
             jax.ShapeDtypeStruct((coeffs, owned), bf16),
             jax.ShapeDtypeStruct((3, leaves, lanes), f32),
         ),
         in_specs=[vmem, vmem, vmem],
-        out_specs=(
-            pl.BlockSpec((coeffs, tile), lambda i: (0, i)),
-            pl.BlockSpec((3, leaves, lanes), lambda i: (0, 0, 0)),
-        ),
-        compiler_params=pltpu.CompilerParams(dimension_semantics=("arbitrary",), vmem_limit_bytes=16 * 1024 * 1024),
+        out_specs=(pl.BlockSpec(memory_space=pl.ANY), vmem),
+        scratch_shapes=[pltpu.VMEM((coeffs, owned), bf16), pltpu.SemaphoreType.DMA((len(parts),))],
+        compiler_params=pltpu.CompilerParams(vmem_limit_bytes=16 * 1024 * 1024),
         name="select",
     )(prod, pick, vel)
     return out_t.T[None], velocity.reshape(1, 3, leaves * lanes)

time: 24 us -> 23.3 us (0.971)
  Pallas kernels: 23.2 us -> 22.5 us
    pallas_call x1, Pallas kernels: 20.3 us -> 19.9 us  [on_device(): pl.pallas_call(functools.partial(exchange_kernel, n_hx, n_nb), out_shape=...]
    pallas_call x1, Pallas kernels: 2.89 us -> 2.57 us  [on_device(): pl.pallas_call(functools.partial(select_kernel, parts), out_shape=(jax.Sh...]
where the time goes in v3:
time: 23.3 us; the launch traced here: 23.2 us
  Pallas kernels  22.5 us (97%)
  between operations  0.64 us (3%)
    pallas_call x1, Pallas kernels, on_device(): pl.pallas_call(functools.partial(exchange_kernel, n_hx, n_nb), out_shape=...  19.9 us
    pallas_call x1, Pallas kernels, on_device(): pl.pallas_call(functools.partial(select_kernel, parts), out_shape=(jax.Sh...  2.57 us

profile of v3, /device:TPU:1, one launch (start us, length us, event | category | flops | bytes accessed | tf_op | source)
XLA Modules:
  0.0 23.2 jit_solution(1953705262477016555)
XLA Ops:
  0.6 19.9 %exchange.1 = (bf16[1464,256]{1,0:T(8,128)(2,1)S(1)}, bf16[256,1024]{1,0:T(8,128)(2,1)S(1)}, f32[3,16,128]{2,1,0:T(8,128)S(1)}) custom-call(s32[1,512]{1,0:T(1,128)} %slots_hbm.1, f32[3,16,128]{2,1,0:T(8,128)} %bitcast.12, f32[3,16,128]{2,1,0:T(8,128)} %bitcast.13, s32[1,16]{1,0:T(1,128)} %counts_hbm.1, s32[8,16]{1,0:T(8,128)} %bitcast.15, ...), custom_call_target="tpu_custom_call" | custom-call | tf_op jit(solution)/shard_map/exchange/pallas_call | solution.py:299
  20.6 2.6 %select.1 = (bf16[1464,1024]{1,0:T(8,128)(2,1)}, f32[3,16,128]{2,1,0:T(8,128)}) custom-call(bf16[1464,256]{1,0:T(8,128)(2,1)S(1)} %get-tuple-element.7.prod_ref, bf16[256,1024]{1,0:T(8,128)(2,1)S(1)} %get-tuple-element.8.pick_ref, f32[3,16,128]{2,1,0:T(8,128)S(1)} %get-tuple-element.9.vel_in), custom_call_target="tpu_custom_call" | custom-call | tf_op jit(solution)/shard_map/select/pallas_call | solution.py:349

commit v4 on v3

--- a/solution.py
+++ b/solution.py
@@ -58,9 +58,9 @@
 
 def exchange_kernel(
     n_hx, n_nb, slots_hbm, pos_hbm, frc_hbm, counts_hbm, nbr_hbm, src_hbm, rows_hbm, ops_hbm,
-    prod_ref, pick_ref, vel_ref,
-    slots_ref, pos_ref, frc_ref, counts_ref, nbr_ref, src_ref,
-    rows, ops, send, recv, gathered, raw, alive, yq, feat, xtgt, moments,
+    gathered, ops, src_ref, vel_ref,
+    slots_ref, pos_ref, frc_ref, counts_ref, nbr_ref,
+    rows, send, recv, raw, alive, yq, feat, xtgt, moments,
     send_sem, recv_sem, halo_send, halo_recv, small_sem, rows_sem, ops_sem,
 ):
     hx, nb = lax.axis_index("hx"), lax.axis_index("nb")
@@ -253,33 +253,42 @@
             rights.append(jnp.where(upper, pltpu.roll(a, UNIQ, 0), b))
         gathered[16 * v : 16 * (v + 1), :half] = jnp.concatenate(lefts, axis=0).astype(bf16)
         gathered[16 * v : 16 * (v + 1), half:] = jnp.concatenate(rights, axis=0).astype(bf16)
-    whose = gathered[:, coeffs : coeffs + 2].astype(f32)
-    ids = (whose[:, 0:1] * 32.0 + whose[:, 1:2]).astype(jnp.int32)
     small[5].wait()
     for c in ops_copies:
         c.wait()
-    for t in range(ops.shape[0]):
-        part = jnp.dot(gathered[:, :coeffs], ops[t], preferred_element_type=f32)
-        prod_ref[:, t * n_keys : (t + 1) * n_keys] = part.T.astype(bf16)
-        pick_ref[t * n_keys : (t + 1) * n_keys, :] = jnp.where(ids == src_ref[t : t + 1, :], 1.0, 0.0).astype(bf16)
-
     for c in chunks:
         c.wait_send()
     up.wait_send()
     down.wait_send()
 
 
-def select_kernel(parts, prod_ref, pick_ref, vel_in, out_hbm, vel_out, buffer, sems):
-    vel_out[...] = vel_in[...]
-    copies, at = [], 0
-    for k, size in enumerate(parts):
-        rows = slice(at, at + size)
-        buffer[rows, :] = jnp.dot(prod_ref[rows, :], pick_ref[...], preferred_element_type=f32).astype(bf16)
+def translate_kernel(parts, rows_ref, ops_ref, src_ref, vel_in, out_hbm, vel_hbm, pick, buffer, sems, vel_sem):
+    vel_copy = pltpu.make_async_copy(vel_in, vel_hbm, vel_sem)
+    vel_copy.start()
+    n_dirs, coeffs = ops_ref.shape[:2]
+    n_keys = rows_ref.shape[0]
+    whose = rows_ref[:, coeffs : coeffs + 2].astype(f32)
+    ids = (whose[:, 0:1] * 32.0 + whose[:, 1:2]).astype(jnp.int32)
+    for t in range(n_dirs):
+        pick[t * n_keys : (t + 1) * n_keys, :] = jnp.where(ids == src_ref[t : t + 1, :], 1.0, 0.0).astype(bf16)
+
+    def product(at, size):
+        held = rows_ref[:, :coeffs]
+        both = [jnp.dot(held, ops_ref[t, :, at : at + size], preferred_element_type=f32) for t in range(n_dirs)]
+        return jnp.concatenate(both, axis=0).T.astype(bf16)
+
+    starts = [sum(parts[:k]) for k in range(len(parts))]
+    copies = []
+    ready = product(0, parts[0])
+    for k, (at, size) in enumerate(zip(starts, parts)):
+        later = product(starts[k + 1], parts[k + 1]) if k + 1 < len(parts) else None
+        buffer[at : at + size, :] = jnp.dot(ready, pick[...], preferred_element_type=f32).astype(bf16)
         copies.append(pltpu.make_async_copy(buffer.at[pl.ds(at, size)], out_hbm.at[pl.ds(at, size)], sems.at[k]))
         copies[-1].start()
-        at += size
+        ready = later
     for c in copies:
         c.wait()
+    vel_copy.wait()
 
 
 def on_device(
@@ -296,27 +305,25 @@
     hbm = pl.BlockSpec(memory_space=pltpu.HBM)
     half = pl.cdiv(coeffs + 8, 256) * 128
     i32 = jnp.int32
-    prod, pick, vel = pl.pallas_call(
+    summed, ops, sources, vel = pl.pallas_call(
         functools.partial(exchange_kernel, n_hx, n_nb),
         out_shape=(
-            jax.ShapeDtypeStruct((coeffs, n_dirs * n_keys), bf16),
-            jax.ShapeDtypeStruct((n_dirs * n_keys, owned), bf16),
+            jax.ShapeDtypeStruct((n_keys, 2 * half), bf16),
+            jax.ShapeDtypeStruct((n_dirs, coeffs, coeffs), bf16),
+            jax.ShapeDtypeStruct((n_dirs, owned), i32),
             jax.ShapeDtypeStruct((3, leaves, lanes), f32),
         ),
         in_specs=[hbm] * 8,
-        out_specs=(vmem, vmem, vmem),
+        out_specs=(vmem, vmem, vmem, vmem),
         scratch_shapes=[
             pltpu.VMEM((1, n_rows), i32),
             pltpu.VMEM((3, leaves, lanes), f32),
             pltpu.VMEM((3, leaves, lanes), f32),
             pltpu.SMEM((1, leaves), i32),
             pltpu.SMEM((n_near, leaves), i32),
-            pltpu.VMEM((n_dirs, owned), i32),
             pltpu.VMEM((2 * half, n_rows), bf16),
-            pltpu.VMEM((n_dirs, coeffs, coeffs), bf16),
             pltpu.VMEM((n_hx, 2 * UNIQ, half), bf16),
             pltpu.VMEM((n_hx, 2 * UNIQ, half), bf16),
-            pltpu.VMEM((n_keys, 2 * half), bf16),
             pltpu.VMEM((3, leaves, 8, lanes), f32),
             pltpu.VMEM((leaves, lanes), f32),
             pltpu.VMEM((3 * leaves, QROWS, lanes), bf16),
@@ -332,7 +339,7 @@
             pltpu.SemaphoreType.DMA((n_dirs,)),
         ],
         compiler_params=pltpu.CompilerParams(
-            collective_id=0, has_side_effects=True, vmem_limit_bytes=48 * 1024 * 1024
+            collective_id=0, has_side_effects=True, vmem_limit_bytes=32 * 1024 * 1024
         ),
         name="exchange",
     )(
@@ -344,20 +351,24 @@
             )
         ]
     )
-    step = pl.cdiv(coeffs, 8 * 8) * 8
-    parts = [min(step, coeffs - k) for k in range(0, coeffs, step)]
+    parts = [min(256, coeffs - k) for k in range(0, coeffs, 256)]
     out_t, velocity = pl.pallas_call(
-        functools.partial(select_kernel, parts),
+        functools.partial(translate_kernel, parts),
         out_shape=(
             jax.ShapeDtypeStruct((coeffs, owned), bf16),
             jax.ShapeDtypeStruct((3, leaves, lanes), f32),
         ),
-        in_specs=[vmem, vmem, vmem],
-        out_specs=(pl.BlockSpec(memory_space=pl.ANY), vmem),
-        scratch_shapes=[pltpu.VMEM((coeffs, owned), bf16), pltpu.SemaphoreType.DMA((len(parts),))],
-        compiler_params=pltpu.CompilerParams(vmem_limit_bytes=16 * 1024 * 1024),
-        name="select",
-    )(prod, pick, vel)
+        in_specs=[vmem] * 4,
+        out_specs=(pl.BlockSpec(memory_space=pl.ANY),) * 2,
+        scratch_shapes=[
+            pltpu.VMEM((n_dirs * n_keys, owned), bf16),
+            pltpu.VMEM((coeffs, owned), bf16),
+            pltpu.SemaphoreType.DMA((len(parts),)),
+            pltpu.SemaphoreType.DMA,
+        ],
+        compiler_params=pltpu.CompilerParams(vmem_limit_bytes=32 * 1024 * 1024),
+        name="translate",
+    )(summed, ops, sources, vel)
     return out_t.T[None], velocity.reshape(1, 3, leaves * lanes)
 
 

time: 23.3 us -> 22.2 us (0.953)
  Pallas kernels: 22.5 us -> 21.5 us
    pallas_call x1, Pallas kernels: 19.9 us -> 18.4 us  [on_device(): pl.pallas_call(functools.partial(exchange_kernel, n_hx, n_nb), out_shape=...]
    pallas_call x1, Pallas kernels: 2.57 us -> 3.1 us  [on_device(): pl.pallas_call(functools.partial(translate_kernel, parts), out_shape=(jax...]
where the time goes in v4:
time: 22.2 us; the launch traced here: 22.1 us
  Pallas kernels  21.5 us (97%)
  between operations  0.64 us (3%)
    pallas_call x1, Pallas kernels, on_device(): pl.pallas_call(functools.partial(exchange_kernel, n_hx, n_nb), out_shape=...  18.4 us
    pallas_call x1, Pallas kernels, on_device(): pl.pallas_call(functools.partial(translate_kernel, parts), out_shape=(jax...  3.1 us

profile of v4, /device:TPU:1, one launch (start us, length us, event | category | flops | bytes accessed | tf_op | source)
XLA Modules:
  0.0 22.1 jit_solution(9540039097708229714)
XLA Ops:
  0.6 18.4 %exchange.1 = (bf16[128,1536]{1,0:T(8,128)(2,1)S(1)}, bf16[2,1464,1464]{2,1,0:T(8,128)(2,1)S(1)}, s32[2,1024]{1,0:T(2,128)S(1)}, f32[3,16,128]{2,1,0:T(8,128)S(1)}) custom-call(s32[1,512]{1,0:T(1,128)} %slots_hbm.1, f32[3,16,128]{2,1,0:T(8,128)} %bitcast.12, f32[3,16,128]{2,1,0:T(8,128)} %bitcast.13, s32[1,16]{1,0:T(1,128)} %counts_hbm.1, s32[8,16]{1,0:T(8,128)} %bitcast.15, ...), custom_call_target="tpu_custom_call" | custom-call | tf_op jit(solution)/shard_map/exchange/pallas_call | solution.py:308
  19.0 3.1 %translate.1 = (bf16[1464,1024]{1,0:T(8,128)(2,1)}, f32[3,16,128]{2,1,0:T(8,128)}) custom-call(bf16[128,1536]{1,0:T(8,128)(2,1)S(1)} %get-tuple-element.8.rows_ref, bf16[2,1464,1464]{2,1,0:T(8,128)(2,1)S(1)} %get-tuple-element.9.ops_ref, s32[2,1024]{1,0:T(2,128)S(1)} %get-tuple-element.10.src_ref, f32[3,16,128]{2,1,0:T(8,128)S(1)} %get-tuple-element.11.vel_in), custom_call_target="tpu_custom_call" | custom-call | tf_op jit(solution)/shard_map/translate/pallas_call | solution.py:355

commit v5 on v4

--- a/solution.py
+++ b/solution.py
@@ -61,10 +61,11 @@
     gathered, ops, src_ref, vel_ref,
     slots_ref, pos_ref, frc_ref, counts_ref, nbr_ref,
     rows, send, recv, raw, alive, yq, feat, xtgt, moments,
-    send_sem, recv_sem, halo_send, halo_recv, small_sem, rows_sem, ops_sem,
+    send_sem, recv_sem, halo_send, halo_recv, ready_sem, news_sem, all_sem, small_sem, rows_sem, ops_sem,
 ):
     hx, nb = lax.axis_index("hx"), lax.axis_index("nb")
-    after, before = lax.rem(nb + 1, n_nb), lax.rem(nb + n_nb - 1, n_nb)
+    after, before = lax.min(nb + 1, n_nb - 1), lax.max(nb - 1, 0)
+    has_after, has_before = nb < n_nb - 1, nb > 0
     coeffs = rows_hbm.shape[0]
     leaves, lanes = pos_ref.shape[1], pos_ref.shape[2]
     half = send.shape[2]
@@ -93,30 +94,18 @@
         return lax.rem(at_x + dx, side) * (2 * side) + lax.rem(at_y + dy, side) * 2 + lax.rem(at_c + dc, 2)
 
     barrier = pltpu.get_barrier_semaphore()
-    for step in steps:
-        pl.semaphore_signal(barrier, inc=1, device_id={"hx": peer(*step)}, device_id_type=MESH)
-    for other in (after, before):
-        pl.semaphore_signal(barrier, inc=1, device_id={"nb": other}, device_id_type=MESH)
+    partner = peer(0, 0, 1)
+    second = at_c == 1
+
+    for dx, dy in sorted({(dx, dy) for dx, dy, _ in steps} - {(0, 0)}, key=lambda c: -sum(min(d, side - d) for d in c)):
+        pl.semaphore_signal(barrier, inc=1, device_id={"hx": peer(dx, dy, 1 - at_c)}, device_id_type=MESH)
+    pl.semaphore_signal(barrier, inc=1, device_id={"hx": partner}, device_id_type=MESH)
+
+    @pl.when(has_after)
+    def _():
+        pl.semaphore_signal(barrier, inc=1, device_id={"hx": hx - at_c, "nb": after}, device_id_type=MESH)
 
     ops_copies = [pltpu.make_async_copy(ops_hbm.at[t], ops.at[t], ops_sem.at[t]) for t in range(ops.shape[0])]
-
-    small[0].wait()
-    slots = slots_ref[...]
-    four = [slots[:, g * lanes : (g + 1) * lanes] for g in range(4)]
-    slots8 = jnp.concatenate(four + four, axis=0)
-    key, first = rank_keys(slots8)
-    key_ids = lax.broadcasted_iota(jnp.int32, (n_keys, lanes), 0)
-    choose = jnp.concatenate(
-        [jnp.where(key_ids == key[g : g + 1, :], 1.0, 0.0).astype(bf16) for g in range(4)], axis=1
-    )
-    high = jnp.where(first, slots8 >> 5, 0).astype(f32)
-    low = jnp.where(first, slots8 & 31, 0).astype(f32)
-    zero6 = jnp.zeros((6, lanes), f32)
-    marks = jnp.concatenate(
-        [jnp.concatenate([high[g : g + 1], low[g : g + 1], zero6], axis=0) for g in range(4)], axis=1
-    )
-    rows[coeffs : coeffs + 8, :] = marks.astype(bf16)
-    rows[coeffs + 8 :, :] = jnp.zeros((rows.shape[0] - coeffs - 8, rows.shape[1]), bf16)
 
     for c in small[1:4]:
         c.wait()
@@ -129,6 +118,59 @@
         block += [jnp.ones((1, lanes), f32), jnp.zeros((1, lanes), f32)]
         raw[1, l] = jnp.concatenate(block, axis=0)
 
+    edge = jnp.zeros((leaves, 8, lanes), f32)
+
+    @pl.when(nb == 0)
+    def _():
+        raw[0] = edge
+
+    @pl.when(nb == n_nb - 1)
+    def _():
+        raw[2] = edge
+
+    def halo(k, target):
+        return pltpu.make_async_remote_copy(
+            src_ref=raw.at[1], dst_ref=raw.at[k], send_sem=halo_send.at[k // 2], recv_sem=halo_recv.at[k // 2],
+            device_id={"nb": target}, device_id_type=MESH,
+        )
+
+    up, down = halo(0, after), halo(2, before)
+
+    @pl.when(jnp.logical_not(second))
+    def _():
+        pl.semaphore_wait(barrier, 1 + 2 * lax.min(nb, 1))
+
+        @pl.when(has_before)
+        def _():
+            pl.semaphore_signal(news_sem, inc=1, device_id={"hx": partner}, device_id_type=MESH)
+
+    @pl.when(has_before)
+    def _():
+        @pl.when(second)
+        def _():
+            pl.semaphore_wait(news_sem, 1)
+
+        down.start()
+        pl.semaphore_signal(ready_sem, inc=1, device_id={"nb": before}, device_id_type=MESH)
+
+    small[0].wait()
+    slots = slots_ref[...]
+    four = [slots[:, g * lanes : (g + 1) * lanes] for g in range(4)]
+    slots8 = jnp.concatenate(four + four, axis=0)
+    key, first = rank_keys(slots8)
+    key_ids = lax.broadcasted_iota(jnp.int32, (n_keys, lanes), 0)
+    choose = jnp.concatenate(
+        [jnp.where(key_ids == key[g : g + 1, :], 1.0, 0.0).astype(bf16) for g in range(4)], axis=1
+    )
+    high = jnp.where(first, slots8 >> 5, 0).astype(f32)
+    low = jnp.where(first, slots8 & 31, 0).astype(f32)
+    zero6 = jnp.zeros((6, lanes), f32)
+    marks = jnp.concatenate(
+        [jnp.concatenate([high[g : g + 1], low[g : g + 1], zero6], axis=0) for g in range(4)], axis=1
+    )
+    rows[coeffs : coeffs + 8, :] = marks.astype(bf16)
+    rows[coeffs + 8 :, :] = jnp.zeros((rows.shape[0] - coeffs - 8, rows.shape[1]), bf16)
+
     rows_copy.wait()
     for c in ops_copies:
         c.start()
@@ -139,29 +181,26 @@
         send[2 * v] = jnp.where(upper, left, pltpu.roll(right, UNIQ, 0)).astype(bf16)
         send[2 * v + 1] = jnp.where(upper, pltpu.roll(left, UNIQ, 0), right).astype(bf16)
 
-    pl.semaphore_wait(barrier, n_hx - 1 + 2)
-
-    def halo(k, target):
-        return pltpu.make_async_remote_copy(
-            src_ref=raw.at[1], dst_ref=raw.at[k], send_sem=halo_send.at[k // 2], recv_sem=halo_recv.at[k // 2],
-            device_id={"nb": target}, device_id_type=MESH,
-        )
-
-    up, down = halo(0, after), halo(2, before)
-    up.start()
-    down.start()
-
-    def chunk(d, step):
+    @pl.when(second)
+    def _():
+        pl.semaphore_wait(barrier, n_hx - 1)
+        pl.semaphore_signal(all_sem, inc=1, device_id={"hx": partner}, device_id_type=MESH)
+
+    @pl.when(jnp.logical_not(second))
+    def _():
+        pl.semaphore_wait(all_sem, 1)
+
+    def chunk(step):
+        place = (step[0] * side + step[1]) * 2 + step[2]
         target = peer(*step)
         return pltpu.make_async_remote_copy(
-            src_ref=send.at[target], dst_ref=recv.at[hx], send_sem=send_sem.at[d], recv_sem=recv_sem.at[d],
+            src_ref=send.at[target], dst_ref=recv.at[place], send_sem=send_sem, recv_sem=recv_sem.at[place // 2],
             device_id={"hx": target}, device_id_type=MESH,
         )
 
-    chunks = [chunk(d, step) for d, step in enumerate(steps)]
-    for c in chunks:
-        c.start()
-    recv[hx] = send[hx]
+    for step in steps:
+        chunk(step).start()
+    recv[0] = send[hx]
 
     row8 = lax.broadcasted_iota(jnp.int32, (leaves, 8, lanes), 1)
     zero8 = jnp.zeros((leaves, 8, lanes), f32)
@@ -187,10 +226,8 @@
     )
     xtgt[...] = jnp.swapaxes(x_table, 1, 2).astype(bf16)
 
-    def source_side(k, mask):
+    def source_side(k):
         src = raw[k]
-        if mask is not None:
-            src = jnp.where(is_frc, src * mask, src)
         at = pl.ds(k * leaves, leaves)
         s_high = rounded(src)
         s_low = rounded(src - s_high)
@@ -213,11 +250,24 @@
         a, b = split3(products), split3(others)
         feat[at] = jnp.concatenate([a[0], b[0], a[1], b[1], a[2], b[2]], axis=1).astype(bf16)
 
-    source_side(1, None)
-    up.wait_recv()
-    source_side(0, jnp.where(nb > 0, 1.0, 0.0).astype(f32))
-    down.wait_recv()
-    source_side(2, jnp.where(nb < n_nb - 1, 1.0, 0.0).astype(f32))
+    source_side(1)
+
+    @pl.when(has_after)
+    def _():
+        pl.semaphore_wait(ready_sem, 1)
+        up.start()
+
+    @pl.when(has_before)
+    def _():
+        up.wait_recv()
+
+    source_side(0)
+
+    @pl.when(has_after)
+    def _():
+        down.wait_recv()
+
+    source_side(2)
     small[4].wait()
 
     def leaf(i, c):
@@ -243,23 +293,33 @@
             u = u - x[b] * (2.0 * m[3 * b + c] + m[3 * c + b])
         vel_ref[c] = u * live
 
-    for c in chunks:
-        c.wait_recv()
-    for v in range(n_hx // 4):
-        lefts, rights = [], []
-        for k in (4 * v, 4 * v + 2):
-            a, b = recv[k].astype(f32), recv[k + 1].astype(f32)
-            lefts.append(jnp.where(upper, a, pltpu.roll(b, UNIQ, 0)))
-            rights.append(jnp.where(upper, pltpu.roll(a, UNIQ, 0), b))
-        gathered[16 * v : 16 * (v + 1), :half] = jnp.concatenate(lefts, axis=0).astype(bf16)
-        gathered[16 * v : 16 * (v + 1), half:] = jnp.concatenate(rights, axis=0).astype(bf16)
+    def arrivals(first, count, sem):
+        part = pl.ds(first, count)
+        return pltpu.make_async_remote_copy(
+            src_ref=send.at[part], dst_ref=recv.at[part], send_sem=send_sem, recv_sem=sem,
+            device_id={"hx": peer(0, 0, 1)}, device_id_type=MESH,
+        )
+
+    chips = sorted({(dx, dy) for dx, dy, _ in steps}, key=lambda c: sum(min(d, side - d) for d in c))
+    for dx, dy in chips:
+        k = dx * side + dy
+        own_chip = 1 if k == 0 else 0
+        arrivals(2 * k + own_chip, 2 - own_chip, recv_sem.at[k]).wait_recv()
+        a, b = recv[2 * k].astype(f32), recv[2 * k + 1].astype(f32)
+        gathered[8 * k : 8 * k + 8, :half] = jnp.where(upper, a, pltpu.roll(b, UNIQ, 0)).astype(bf16)
+        gathered[8 * k : 8 * k + 8, half:] = jnp.where(upper, pltpu.roll(a, UNIQ, 0), b).astype(bf16)
     small[5].wait()
     for c in ops_copies:
         c.wait()
-    for c in chunks:
-        c.wait_send()
-    up.wait_send()
-    down.wait_send()
+    arrivals(0, n_hx - 1, recv_sem.at[0]).wait_send()
+
+    @pl.when(has_after)
+    def _():
+        up.wait_send()
+
+    @pl.when(has_before)
+    def _():
+        down.wait_send()
 
 
 def translate_kernel(parts, rows_ref, ops_ref, src_ref, vel_in, out_hbm, vel_hbm, pick, buffer, sems, vel_sem):
@@ -330,10 +390,13 @@
             pltpu.VMEM((3 * leaves, FROWS, lanes), bf16),
             pltpu.VMEM((leaves, lanes, QROWS), bf16),
             pltpu.VMEM((leaves, 16, lanes), f32),
-            pltpu.SemaphoreType.DMA((n_hx,)),
-            pltpu.SemaphoreType.DMA((n_hx,)),
+            pltpu.SemaphoreType.DMA,
+            pltpu.SemaphoreType.DMA((n_hx // 2,)),
             pltpu.SemaphoreType.DMA((2,)),
             pltpu.SemaphoreType.DMA((2,)),
+            pltpu.SemaphoreType.REGULAR,
+            pltpu.SemaphoreType.REGULAR,
+            pltpu.SemaphoreType.REGULAR,
             pltpu.SemaphoreType.DMA((6,)),
             pltpu.SemaphoreType.DMA,
             pltpu.SemaphoreType.DMA((n_dirs,)),

time: 22.2 us -> 17.4 us (0.78)
  Pallas kernels: 21.5 us -> 16.7 us
    pallas_call x1, Pallas kernels: 18.4 us -> 13.6 us  [on_device(): pl.pallas_call(functools.partial(exchange_kernel, n_hx, n_nb), out_shape=...]
where the time goes in v5:
time: 17.4 us; the launch traced here: 17.3 us
  Pallas kernels  16.7 us (96%)
  between operations  0.64 us (4%)
    pallas_call x1, Pallas kernels, on_device(): pl.pallas_call(functools.partial(exchange_kernel, n_hx, n_nb), out_shape=...  13.6 us
    pallas_call x1, Pallas kernels, on_device(): pl.pallas_call(functools.partial(translate_kernel, parts), out_shape=(jax...  3.1 us

profile of v5, /device:TPU:1, one launch (start us, length us, event | category | flops | bytes accessed | tf_op | source)
XLA Modules:
  0.0 17.3 jit_solution(15960341999269988114)
XLA Ops:
  0.6 13.6 %exchange.1 = (bf16[128,1536]{1,0:T(8,128)(2,1)S(1)}, bf16[2,1464,1464]{2,1,0:T(8,128)(2,1)S(1)}, s32[2,1024]{1,0:T(2,128)S(1)}, f32[3,16,128]{2,1,0:T(8,128)S(1)}) custom-call(s32[1,512]{1,0:T(1,128)} %slots_hbm.1, f32[3,16,128]{2,1,0:T(8,128)} %bitcast.12, f32[3,16,128]{2,1,0:T(8,128)} %bitcast.13, s32[1,16]{1,0:T(1,128)} %counts_hbm.1, s32[8,16]{1,0:T(8,128)} %bitcast.15, ...), custom_call_target="tpu_custom_call" | custom-call | tf_op jit(solution)/shard_map/exchange/pallas_call | solution.py:368
  14.2 3.1 %translate.1 = (bf16[1464,1024]{1,0:T(8,128)(2,1)}, f32[3,16,128]{2,1,0:T(8,128)}) custom-call(bf16[128,1536]{1,0:T(8,128)(2,1)S(1)} %get-tuple-element.8.rows_ref, bf16[2,1464,1464]{2,1,0:T(8,128)(2,1)S(1)} %get-tuple-element.9.ops_ref, s32[2,1024]{1,0:T(2,128)S(1)} %get-tuple-element.10.src_ref, f32[3,16,128]{2,1,0:T(8,128)S(1)} %get-tuple-element.11.vel_in), custom_call_target="tpu_custom_call" | custom-call | tf_op jit(solution)/shard_map/translate/pallas_call | solution.py:418

commit v6 on v5

--- a/solution.py
+++ b/solution.py
@@ -172,8 +172,6 @@
     rows[coeffs + 8 :, :] = jnp.zeros((rows.shape[0] - coeffs - 8, rows.shape[1]), bf16)
 
     rows_copy.wait()
-    for c in ops_copies:
-        c.start()
     sums = lax.dot_general(choose, rows[...], NT_DIMS, preferred_element_type=f32)
     upper = lax.broadcasted_iota(jnp.int32, (8, half), 0) < UNIQ
     for v in range(n_hx // 2):
@@ -201,6 +199,8 @@
     for step in steps:
         chunk(step).start()
     recv[0] = send[hx]
+    for c in ops_copies:
+        c.start()
 
     row8 = lax.broadcasted_iota(jnp.int32, (leaves, 8, lanes), 1)
     zero8 = jnp.zeros((leaves, 8, lanes), f32)

time: 17.4 us -> 17.4 us (level)
  no operation moved by 1% of the time
where the time goes in v6:
time: 17.4 us; the launch traced here: 17.3 us
  Pallas kernels  16.7 us (96%)
  between operations  0.64 us (4%)
    pallas_call x1, Pallas kernels, on_device(): pl.pallas_call(functools.partial(exchange_kernel, n_hx, n_nb), out_shape=...  13.6 us
    pallas_call x1, Pallas kernels, on_device(): pl.pallas_call(functools.partial(translate_kernel, parts), out_shape=(jax...  3.1 us

profile of v6, /device:TPU:1, one launch (start us, length us, event | category | flops | bytes accessed | tf_op | source)
XLA Modules:
  0.0 17.3 jit_solution(1148240575505157753)
XLA Ops:
  0.6 13.6 %exchange.1 = (bf16[128,1536]{1,0:T(8,128)(2,1)S(1)}, bf16[2,1464,1464]{2,1,0:T(8,128)(2,1)S(1)}, s32[2,1024]{1,0:T(2,128)S(1)}, f32[3,16,128]{2,1,0:T(8,128)S(1)}) custom-call(s32[1,512]{1,0:T(1,128)} %slots_hbm.1, f32[3,16,128]{2,1,0:T(8,128)} %bitcast.12, f32[3,16,128]{2,1,0:T(8,128)} %bitcast.13, s32[1,16]{1,0:T(1,128)} %counts_hbm.1, s32[8,16]{1,0:T(8,128)} %bitcast.15, ...), custom_call_target="tpu_custom_call" | custom-call | tf_op jit(solution)/shard_map/exchange/pallas_call | solution.py:368
  14.2 3.1 %translate.1 = (bf16[1464,1024]{1,0:T(8,128)(2,1)}, f32[3,16,128]{2,1,0:T(8,128)}) custom-call(bf16[128,1536]{1,0:T(8,128)(2,1)S(1)} %get-tuple-element.8.rows_ref, bf16[2,1464,1464]{2,1,0:T(8,128)(2,1)S(1)} %get-tuple-element.9.ops_ref, s32[2,1024]{1,0:T(2,128)S(1)} %get-tuple-element.10.src_ref, f32[3,16,128]{2,1,0:T(8,128)S(1)} %get-tuple-element.11.vel_in), custom_call_target="tpu_custom_call" | custom-call | tf_op jit(solution)/shard_map/translate/pallas_call | solution.py:418

commit v7 on v6

--- a/solution.py
+++ b/solution.py
@@ -300,7 +300,7 @@
             device_id={"hx": peer(0, 0, 1)}, device_id_type=MESH,
         )
 
-    chips = sorted({(dx, dy) for dx, dy, _ in steps}, key=lambda c: sum(min(d, side - d) for d in c))
+    chips = sorted({(dx, dy) for dx, dy, _ in steps}, key=lambda c: -sum(min(d, side - d) for d in c))
     for dx, dy in chips:
         k = dx * side + dy
         own_chip = 1 if k == 0 else 0

time: 17.4 us -> 17.3 us (level)
  no operation moved by 1% of the time
where the time goes in v7:
time: 17.3 us; the launch traced here: 17.2 us
  Pallas kernels  16.6 us (96%)
  between operations  0.64 us (4%)
    pallas_call x1, Pallas kernels, on_device(): pl.pallas_call(functools.partial(exchange_kernel, n_hx, n_nb), out_shape=...  13.5 us
    pallas_call x1, Pallas kernels, on_device(): pl.pallas_call(functools.partial(translate_kernel, parts), out_shape=(jax...  3.1 us

profile of v7, /device:TPU:1, one launch (start us, length us, event | category | flops | bytes accessed | tf_op | source)
XLA Modules:
  0.0 17.2 jit_solution(10365120214951199917)
XLA Ops:
  0.6 13.5 %exchange.1 = (bf16[128,1536]{1,0:T(8,128)(2,1)S(1)}, bf16[2,1464,1464]{2,1,0:T(8,128)(2,1)S(1)}, s32[2,1024]{1,0:T(2,128)S(1)}, f32[3,16,128]{2,1,0:T(8,128)S(1)}) custom-call(s32[1,512]{1,0:T(1,128)} %slots_hbm.1, f32[3,16,128]{2,1,0:T(8,128)} %bitcast.12, f32[3,16,128]{2,1,0:T(8,128)} %bitcast.13, s32[1,16]{1,0:T(1,128)} %counts_hbm.1, s32[8,16]{1,0:T(8,128)} %bitcast.15, ...), custom_call_target="tpu_custom_call" | custom-call | tf_op jit(solution)/shard_map/exchange/pallas_call | solution.py:368
  14.1 3.1 %translate.1 = (bf16[1464,1024]{1,0:T(8,128)(2,1)}, f32[3,16,128]{2,1,0:T(8,128)}) custom-call(bf16[128,1536]{1,0:T(8,128)(2,1)S(1)} %get-tuple-element.8.rows_ref, bf16[2,1464,1464]{2,1,0:T(8,128)(2,1)S(1)} %get-tuple-element.9.ops_ref, s32[2,1024]{1,0:T(2,128)S(1)} %get-tuple-element.10.src_ref, f32[3,16,128]{2,1,0:T(8,128)S(1)} %get-tuple-element.11.vel_in), custom_call_target="tpu_custom_call" | custom-call | tf_op jit(solution)/shard_map/translate/pallas_call | solution.py:418
